TPU v7x, 32 devices: a whole 2x2x4 slice. The times are simulated.
32 devices in a mesh: row: 2 (over x), feat: 16 (over z, y, core).
Axes of the slice: x: 2, y: 2, z: 4, core: 2. Of those that a mesh axis runs over, the one named last changes fastest.
Arguments:
- logits: bfloat16 [2048, 1000], P(('row', 'feat')), may hold values from -200 to 200, as said below
- labels: int32 [2048], P(('row', 'feat')), may hold values from 0 to 999
- projection: bfloat16 [1000, 16], replicated, may hold values from -4 to 4
- bins: int32 [2048, 2048], P('feat', 'row'), may hold values from 0 to 63, as said below
- nbins: int32 [2048], P('feat'), may hold values from 2 to 64
- leaf: int32 [2048], P('row'), may hold values from 0 to 15
Outputs:
- relative_gain: float32 [16, 131072], P('row', 'feat')
Inputs may be any that keep to these rules, and one draw needn't show every extreme that they name: `logits`: shows the class scores; some rows may lie far from zero. bins[f, i] < nbins[f].
All inputs are finite; a program needn't handle non-finite values.
Results may differ from a plain program's by a relative error of at most 0.0017.
Values may be sent and summed in bfloat16 or wider, within the bound.
No kernel may reach another device: no remote copies, remote signals or barrier semaphores. Data moves between devices by JAX's collectives and lax.ppermute only.
A program may use at most 64 MiB of HBM per device.

v0:
```python
import functools

import jax
import jax.numpy as jnp
from jax import lax
from jax.experimental import pallas as pl
from jax.experimental.pallas import tpu as pltpu
from jax.sharding import PartitionSpec as P


BINS = 64
LEAVES = 16
LANES = 128
STEPS = 4
ridge = 1.0
epsilon = 1e-06


def vmem():
    return pl.BlockSpec(memory_space=pltpu.VMEM)


def lanes_of(features):
    return features * max(1, LANES // features)


def prepare_kernel(bins_hbm, leaf_hbm, logits_hbm, labels_hbm, projection_hbm, turned_ref, values_ref, *scratch):
    bins_ref, leaf_ref, logits_ref, labels_ref, projection_ref, arrived = scratch
    pairs = (
        (logits_hbm, logits_ref),
        (labels_hbm, labels_ref),
        (projection_hbm, projection_ref),
        (bins_hbm, bins_ref),
        (leaf_hbm, leaf_ref),
    )
    arrivals = [pltpu.make_async_copy(a, b, arrived.at[i]) for i, (a, b) in enumerate(pairs)]
    for arrival in arrivals:
        arrival.start()
    for arrival in arrivals[:3]:
        arrival.wait()

    rows, classes = logits_ref.shape
    scores = logits_ref[...].astype(jnp.float32)
    highest = jnp.max(scores, axis=1, keepdims=True)
    expd = jnp.exp(scores - highest)
    probability = expd / jnp.sum(expd, axis=1, keepdims=True)
    labels = jnp.broadcast_to(labels_ref[...].astype(jnp.float32), (LANES, rows))
    labels = jnp.transpose(labels)[:, :1].astype(jnp.int32)
    lane = lax.broadcasted_iota(jnp.int32, (rows, classes), 1)
    target = jnp.where(lane == labels, 1.0, 0.0)
    gradient = (probability - target).astype(jnp.bfloat16)
    sketch = lax.dot_general(
        projection_ref[...], gradient, (((1,), (1,)), ((), ())), preferred_element_type=jnp.float32
    )
    hessian = jnp.sum(probability * (1.0 - probability), axis=1, keepdims=True)
    hessian = jnp.transpose(jnp.broadcast_to(hessian, (rows, LANES)))[:8, :]
    top = jnp.concatenate([sketch[:8], hessian], axis=0)
    low = jnp.concatenate([sketch[8:], jnp.zeros_like(hessian)], axis=0)
    packed = jnp.concatenate([top, low], axis=1).astype(jnp.bfloat16)
    values_ref[...] = jnp.broadcast_to(packed[None], values_ref.shape)

    for arrival in arrivals[3:]:
        arrival.wait()
    lines = bins_ref.shape[1]
    turned = jnp.transpose(bins_ref[...].astype(jnp.float32))
    copies = turned_ref.shape[1] // bins_ref.shape[0]
    if copies > 1:
        turned = jnp.concatenate([turned] * copies, axis=1)
    turned_ref[:lines, :] = turned.astype(jnp.bfloat16)
    leaf = leaf_ref[...].astype(jnp.float32)
    spare = turned_ref.shape[0] - lines - leaf.shape[0]
    leaf = jnp.concatenate([leaf, jnp.zeros((spare, LANES), jnp.float32)], axis=0) if spare else leaf
    turned_ref[lines:, :LANES] = leaf.astype(jnp.bfloat16)


def prepare(bins, leaf, logits, labels, projection, destinations):
    features, lines = bins.shape
    rows = logits.shape[0]
    tail = -(-lines // LANES // 16) * 16
    given = (bins, leaf.reshape(lines // LANES, LANES), logits, labels.reshape(1, rows), projection.T)
    return pl.pallas_call(
        prepare_kernel,
        out_shape=(
            jax.ShapeDtypeStruct((lines + tail, lanes_of(features)), jnp.bfloat16),
            jax.ShapeDtypeStruct((destinations, 16, 2 * rows), jnp.bfloat16),
        ),
        in_specs=[pl.BlockSpec(memory_space=pltpu.HBM)] * 5,
        out_specs=(vmem(), vmem()),
        scratch_shapes=[pltpu.VMEM(x.shape, x.dtype) for x in given] + [pltpu.SemaphoreType.DMA((5,))],
        compiler_params=pltpu.CompilerParams(vmem_limit_bytes=16 << 20),
        name="prepare",
    )(*[pltpu.with_memory_space_constraint(x, pltpu.HBM) for x in given])


def gain_kernel(n_row, share, features, steps, values_ref, nbins_ref, *refs):
    bins_refs, (gain_ref, best_ref), (weights,) = refs[:n_row], refs[n_row : n_row + 2], refs[n_row + 2 :]
    width = bins_refs[0].shape[1]
    sources = values_ref.shape[0] // n_row
    half = values_ref.shape[2] // 2
    rows = sources * half
    me = lax.axis_index("row")
    wide = (share, LANES)
    my_leaf = lax.broadcasted_iota(jnp.int32, wide, 0) + me * share
    my_leaf = my_leaf.astype(jnp.float32)
    left_half = lax.broadcasted_iota(jnp.int32, (16, LANES), 1) < half
    totals = [jnp.zeros(wide, jnp.float32) for _ in range(17)]
    for s in range(n_row):
        shard = lax.rem(me + s, n_row)
        for pair in range(sources // 2):
            first = values_ref[shard * sources + 2 * pair].astype(jnp.float32)
            second = values_ref[shard * sources + 2 * pair + 1].astype(jnp.float32)
            top = jnp.where(left_half, first, pltpu.roll(second, half, 1))
            low = jnp.where(left_half, pltpu.roll(first, half, 1), second)
            at = rows + pair // 16 * 16
            leaf = bins_refs[s][at : at + 16, :LANES].astype(jnp.float32)[pair % 16 : pair % 16 + 1]
            mine = jnp.broadcast_to(leaf, wide) == my_leaf
            pieces = []
            for k in range(17):
                row = top[k : k + 1] if k < 8 else low[k - 8 : k - 7] if k < 16 else top[8:9]
                piece = jnp.where(mine, jnp.broadcast_to(row, wide), 0.0)
                totals[k] = totals[k] + piece
                pieces.append(piece)
            spare = -(-17 * share // 16) * 16 - 17 * share
            if spare:
                pieces.append(jnp.zeros((spare, LANES), jnp.float32))
            weights[:, s * rows + pair * LANES : s * rows + (pair + 1) * LANES] = jnp.concatenate(
                pieces, axis=0
            ).astype(jnp.bfloat16)
    full = (share, width)
    totals = [jnp.broadcast_to(jnp.sum(t, axis=1, keepdims=True), full) for t in totals]

    def score(sums):
        squares = sums[0] * sums[0]
        for k in range(1, 16):
            squares = squares + sums[k] * sums[k]
        return squares / (sums[16] + ridge)

    of_all = score(totals)
    copies = width // features
    bin_of = lax.broadcasted_iota(jnp.int32, (1, width), 1) // features
    last = jnp.broadcast_to(nbins_ref[...] - 1, full)
    one, zero = jnp.bfloat16(1.0), jnp.bfloat16(0.0)

    def add_group(g, best):
        sums = None
        ids = [bin_of + (g * steps + j) * copies for j in range(steps)]
        for s in range(n_row):
            table = bins_refs[s][:rows, :]
            tables = jnp.concatenate(
                [jnp.where(table <= i.astype(jnp.float32).astype(jnp.bfloat16), one, zero) for i in ids], axis=1
            )
            part = lax.dot_general(
                weights[:, s * rows : (s + 1) * rows],
                tables,
                (((1,), (0,)), ((), ())),
                preferred_element_type=jnp.float32,
            )
            sums = part if sums is None else sums + part
        for j in range(steps):
            left = [sums[k * share : (k + 1) * share, j * width : (j + 1) * width] for k in range(17)]
            right = [totals[k] - left[k] for k in range(17)]
            gain = score(left) + score(right) - of_all
            gain = jnp.where(jnp.broadcast_to(ids[j], full) < last, gain, 0.0)
            gain_ref[g * steps + j] = gain
            best = jnp.maximum(best, gain)
        return best

    count = BINS // copies // steps
    best = lax.fori_loop(0, count, add_group, jnp.full(full, -jnp.inf, jnp.float32))
    best_ref[...] = jnp.broadcast_to(jnp.max(best, axis=1, keepdims=True), wide)


def split_gains(values, nbins, bins, n_row):
    share = LEAVES // n_row
    features = nbins.shape[0]
    width = bins[0].shape[1]
    copies = width // features
    rows = values.shape[0] // n_row * values.shape[2] // 2
    return pl.pallas_call(
        functools.partial(gain_kernel, n_row, share, features, STEPS),
        out_shape=(
            jax.ShapeDtypeStruct((BINS // copies, share, width), jnp.float32),
            jax.ShapeDtypeStruct((share, LANES), jnp.float32),
        ),
        in_specs=[vmem()] * (2 + n_row),
        out_specs=(vmem(), vmem()),
        scratch_shapes=[pltpu.VMEM((-(-17 * share // 16) * 16, n_row * rows), jnp.bfloat16)],
        compiler_params=pltpu.CompilerParams(vmem_limit_bytes=16 << 20),
        name="gains",
    )(values, jnp.tile(nbins, copies).reshape(1, width), *bins)


def max_over(x, axis, size):
    step = 1
    while step < size:
        x = jnp.maximum(x, lax.ppermute(x, axis, [(i, i ^ step) for i in range(size)]))
        step *= 2
    return x


def on_device(n_row, n_feat, logits, labels, projection, bins, nbins, leaf):
    own, copies = prepare(bins, leaf, logits, labels, projection, n_row * n_feat)
    values = lax.all_to_all(copies, ("row", "feat"), 0, 0)
    all_bins = [own]
    for s in range(1, n_row):
        all_bins.append(lax.ppermute(own, "row", [((i + s) % n_row, i) for i in range(n_row)]))
    gain, best = split_gains(values, nbins, all_bins, n_row)
    best = max_over(best, "feat", n_feat)
    share, features = best.shape[0], bins.shape[0]
    gain = gain.transpose(1, 0, 2).reshape(share, BINS, features).transpose(0, 2, 1)
    return gain.reshape(share, features * BINS) / (best[:, :1] + epsilon)


def solution(mesh):
    return jax.shard_map(
        functools.partial(on_device, mesh.shape["row"], mesh.shape["feat"]),
        mesh=mesh,
        in_specs=(
            P(("row", "feat"), None),
            P(("row", "feat")),
            P(),
            P("feat", "row"),
            P("feat"),
            P("row"),
        ),
        out_specs=P("row", "feat"),
        check_vma=False,
    )
```

profile of v0, /device:TPU:0, one launch (start us, length us, event | category | flops | bytes accessed | tf_op | source)
XLA Modules:
  0.0 41.3 jit_solution(13642953284291456145)
XLA Ops:
  0.0 1.6 %prepare.1 = (bf16[1040,128]{1,0:T(8,128)(2,1)S(1)}, bf16[32,16,128]{2,1,0:T(8,128)(2,1)S(1)}) custom-call(s32[128,1024]{1,0:T(8,128)} %bins_hbm.1, s32[8,128]{1,0:T(8,128)} %bitcast.8, bf16[64,1000]{1,0:T(8,128)(2,1)} %logits_hbm.1, s32[1,64]{1,0:T(1,128)} %bitcast.9, bf16[16,1000]{1,0:T(8,128)(2,1)} %bitcast.7), custom_call_target="tpu_custom_call" | custom-call | tf_op jit(solution)/shard_map/prepare/pallas_call | solution.py:81
  1.6 3.0 %collective-permute-start = (bf16[1040,128]{1,0:T(8,128)(2,1)S(1)}, bf16[1040,128]{1,0:T(8,128)(2,1)S(1)}, u32[]{:S(2)}, u32[]{:S(2)}) collective-permute-start(bf16[1040,128]{1,0:T(8,128)(2,1)S(1)} %get-tuple-element.10.refs_0_), channel_id=1, source_target_pairs={{16,0},{0,16},{17,1},{1,17},{18,2},{2,18},{19,3},{3,19},{20,4},{4,... | collective-permute-start | bytes 798728 | tf_op jit(solution)/shard_map/ppermute | solution.py:206
  4.6 12.9 %all_to_all.5.values_ref = bf16[32,16,128]{2,1,0:T(8,128)(2,1)S(1)} all-to-all(bf16[32,16,128]{2,1,0:T(8,128)(2,1)S(1)} %get-tuple-element.9), channel_id=1, replica_groups=mesh['row'=2,'feat'=16] {'row','feat'}, dimensions={0} | all-to-all | bytes 262144 | tf_op jit(solution)/shard_map/all_to_all | solution.py:203
  17.5 0.0 copy-start
  17.5 0.0 collective-permute-done.refs_1_
  17.5 0.7 %copy-done = s32[128]{0:T(128)S(1)} copy-done((s32[128]{0:T(128)S(1)}, s32[128]{0:T(128)}, u32[]{:S(2)}) %copy-start) | copy-done | bytes 536
  18.2 9.3 %gains.1 = (f32[64,8,128]{2,1,0:T(8,128)S(1)}, f32[8,128]{1,0:T(8,128)S(1)}) custom-call(bf16[32,16,128]{2,1,0:T(8,128)(2,1)S(1)} %all_to_all.5.values_ref, s32[1,128]{1,0:T(1,128)S(1)} %bitcast.6, bf16[1040,128]{1,0:T(8,128)(2,1)S(1)} %get-tuple-element.10.refs_0_, bf16[1040,128]{1,0:T(8,128)(2,1)S(1)} %collective-permute-done.refs_1_), custom_call_target="tpu_custom_call" | custom-call | tf_op jit(solution)/shard_map/gains/pallas_call | solution.py:179
  27.5 0.3 collective-permute-start.1
  27.8 0.9 %collective-permute-done.1 = f32[8,128]{1,0:T(8,128)S(1)} collective-permute-done((f32[8,128]{1,0:T(8,128)S(1)}, f32[8,128]{1,0:T(8,128)S(1)}, u32[]{:S(2)}, u32[]{:S(2)}) %collective-permute-start.1) | collective-permute-done | bytes 4128 | tf_op jit(solution)/shard_map/ppermute | solution.py:196
  28.7 0.4 %collective-permute-start.2 = (f32[8,128]{1,0:T(8,128)S(1)}, f32[8,128]{1,0:T(8,128)S(1)}, u32[]{:S(2)}, u32[]{:S(2)}) collective-permute-start(f32[8,128]{1,0:T(8,128)S(1)} %max.12), channel_id=1, source_target_pairs={{0,2},{1,3},{2,0},{3,1},{4,6},{5,7},{6,4},{7,5},{8,10},{9,11},{10,... | collective-permute-start | bytes 12296 | tf_op jit(solution)/shard_map/ppermute | solution.py:196
  29.1 3.2 %collective-permute-done.2 = f32[8,128]{1,0:T(8,128)S(1)} collective-permute-done((f32[8,128]{1,0:T(8,128)S(1)}, f32[8,128]{1,0:T(8,128)S(1)}, u32[]{:S(2)}, u32[]{:S(2)}) %collective-permute-start.2) | collective-permute-done | bytes 4128 | tf_op jit(solution)/shard_map/ppermute | solution.py:196
  32.3 0.0 collective-permute-start.3
  32.3 3.6 %collective-permute-done.3 = f32[8,128]{1,0:T(8,128)S(1)} collective-permute-done((f32[8,128]{1,0:T(8,128)S(1)}, f32[8,128]{1,0:T(8,128)S(1)}, u32[]{:S(2)}, u32[]{:S(2)}) %collective-permute-start.3) | collective-permute-done | bytes 4128 | tf_op jit(solution)/shard_map/ppermute | solution.py:196
  35.9 0.7 %collective-permute-start.4 = (f32[8,128]{1,0:T(8,128)S(1)}, f32[8,128]{1,0:T(8,128)S(1)}, u32[]{:S(2)}, u32[]{:S(2)}) collective-permute-start(f32[8,128]{1,0:T(8,128)S(1)} %max.14), channel_id=1, source_target_pairs={{0,8},{1,9},{2,10},{3,11},{4,12},{5,13},{6,14},{7,15},{8,0},{9,1},... | collective-permute-start | bytes 12296 | tf_op jit(solution)/shard_map/ppermute | solution.py:196
  36.6 0.2 copy.7
  36.8 0.2 reshape.11
  37.0 3.4 %collective-permute-done.4 = f32[8,128]{1,0:T(8,128)S(1)} collective-permute-done((f32[8,128]{1,0:T(8,128)S(1)}, f32[8,128]{1,0:T(8,128)S(1)}, u32[]{:S(2)}, u32[]{:S(2)}) %collective-permute-start.4) | collective-permute-done | bytes 4128 | tf_op jit(solution)/shard_map/ppermute | solution.py:196
  40.4 0.1 add_reduce_fusion
  40.5 0.8 %broadcast_divide_fusion = f32[8,8192]{1,0:T(8,128)} fusion(f32[8,8192]{1,0:T(8,128)S(1)} %reshape.11, f32[8]{0:T(128)S(1)} %add_reduce_fusion), kind=kLoop, calls=%fused_computation | loop fusion | flops 65536 | bytes 524320 | tf_op jit(solution)/shard_map/div | solution.py:211
  (4 shorter events, 0.0 us)
Async XLA Ops:
  1.6 16.0 %collective-permute-start = (bf16[1040,128]{1,0:T(8,128)(2,1)S(1)}, bf16[1040,128]{1,0:T(8,128)(2,1)S(1)}, u32[]{:S(2)}, u32[]{:S(2)}) collective-permute-start(bf16[1040,128]{1,0:T(8,128)(2,1)S(1)} %get-tuple-element.10.refs_0_), channel_id=1, source_target_pairs={{16,0},{0,16},{17,1},{1,17},{18,2},{2,18},{19,3},{3,19},{20,4},{4,... | collective-permute-start | bytes 798728 | tf_op jit(solution)/shard_map/ppermute | solution.py:206
  17.5 0.7 %copy-start = (s32[128]{0:T(128)S(1)}, s32[128]{0:T(128)}, u32[]{:S(2)}) copy-start(s32[128]{0:T(128)} %param.10) | copy-start | bytes 1540
  27.5 1.2 %collective-permute-start.1 = (f32[8,128]{1,0:T(8,128)S(1)}, f32[8,128]{1,0:T(8,128)S(1)}, u32[]{:S(2)}, u32[]{:S(2)}) collective-permute-start(f32[8,128]{1,0:T(8,128)S(1)} %get-tuple-element.12), channel_id=1, source_target_pairs={{0,1},{1,0},{2,3},{3,2},{4,5},{5,4},{6,7},{7,6},{8,9},{9,8},{10,11... | collective-permute-start | bytes 12296 | tf_op jit(solution)/shard_map/ppermute | solution.py:196
  28.7 3.6 %collective-permute-start.2 = (f32[8,128]{1,0:T(8,128)S(1)}, f32[8,128]{1,0:T(8,128)S(1)}, u32[]{:S(2)}, u32[]{:S(2)}) collective-permute-start(f32[8,128]{1,0:T(8,128)S(1)} %max.12), channel_id=1, source_target_pairs={{0,2},{1,3},{2,0},{3,1},{4,6},{5,7},{6,4},{7,5},{8,10},{9,11},{10,... | collective-permute-start | bytes 12296 | tf_op jit(solution)/shard_map/ppermute | solution.py:196
  32.3 3.6 %collective-permute-start.3 = (f32[8,128]{1,0:T(8,128)S(1)}, f32[8,128]{1,0:T(8,128)S(1)}, u32[]{:S(2)}, u32[]{:S(2)}) collective-permute-start(f32[8,128]{1,0:T(8,128)S(1)} %max.13), channel_id=1, source_target_pairs={{0,4},{1,5},{2,6},{3,7},{4,0},{5,1},{6,2},{7,3},{8,12},{9,13},{10,... | collective-permute-start | bytes 12296 | tf_op jit(solution)/shard_map/ppermute | solution.py:196
  35.9 4.5 %collective-permute-start.4 = (f32[8,128]{1,0:T(8,128)S(1)}, f32[8,128]{1,0:T(8,128)S(1)}, u32[]{:S(2)}, u32[]{:S(2)}) collective-permute-start(f32[8,128]{1,0:T(8,128)S(1)} %max.14), channel_id=1, source_target_pairs={{0,8},{1,9},{2,10},{3,11},{4,12},{5,13},{6,14},{7,15},{8,0},{9,1},... | collective-permute-start | bytes 12296 | tf_op jit(solution)/shard_map/ppermute | solution.py:196
where the time goes:
time: 41.5 us; the launch traced here: 41.3 us
  blocking collectives  12.9 us (31%)
  waiting for transfers between devices  11.1 us (27%)
  Pallas kernels  10.9 us (26%)
  starting transfers between devices  4.45 us (11%)
  local copies, waits for them, and re-layouts  1.05 us (3%)
  other arithmetic  0.93 us (2%)
    all_to_all x1, blocking collectives, on_device(): values = lax.all_to_all(copies, ('row', 'feat'), 0, 0)  12.9 us
    ppermute x4, waiting for transfers between devices, max_over(): lax.ppermute(x, axis, [(i, i ^ step) for i in range(size)])  11.1 us
    pallas_call x1, Pallas kernels, split_gains(): pl.pallas_call(functools.partial(gain_kernel, n_row, share, features, STE...  9.31 us
    ppermute x1, starting transfers between devices, on_device(): lax.ppermute(own, 'row', [((i + s) % n_row, i) for i in range(n_row)])  3.03 us
    pallas_call x1, Pallas kernels, prepare(): pl.pallas_call(prepare_kernel, out_shape=(jax.ShapeDtypeStruct((lines + t...  1.57 us
    ppermute x4, starting transfers between devices, max_over(): lax.ppermute(x, axis, [(i, i ^ step) for i in range(size)])  1.42 us
  transfers between devices with their start and end apart: 5, of which 4 were waited for; matrix products, arithmetic and copies ran while one was open for 1% of the time, Pallas kernels for 0%

commit v1 on v0

--- a/solution.py
+++ b/solution.py
@@ -11,7 +11,7 @@
 BINS = 64
 LEAVES = 16
 LANES = 128
-STEPS = 4
+STEPS = 16
 ridge = 1.0
 epsilon = 1e-06
 
@@ -93,7 +93,7 @@
 
 
 def gain_kernel(n_row, share, features, steps, values_ref, nbins_ref, *refs):
-    bins_refs, (gain_ref, best_ref), (weights,) = refs[:n_row], refs[n_row : n_row + 2], refs[n_row + 2 :]
+    bins_refs, (gain_ref, best_ref), (weights, wide_bins) = refs[:n_row], refs[n_row : n_row + 2], refs[n_row + 2 :]
     width = bins_refs[0].shape[1]
     sources = values_ref.shape[0] // n_row
     half = values_ref.shape[2] // 2
@@ -126,6 +126,7 @@
             weights[:, s * rows + pair * LANES : s * rows + (pair + 1) * LANES] = jnp.concatenate(
                 pieces, axis=0
             ).astype(jnp.bfloat16)
+        wide_bins[s * rows : (s + 1) * rows, :] = bins_refs[s][:rows, :].astype(jnp.float32)
     full = (share, width)
     totals = [jnp.broadcast_to(jnp.sum(t, axis=1, keepdims=True), full) for t in totals]
 
@@ -142,20 +143,12 @@
     one, zero = jnp.bfloat16(1.0), jnp.bfloat16(0.0)
 
     def add_group(g, best):
-        sums = None
         ids = [bin_of + (g * steps + j) * copies for j in range(steps)]
-        for s in range(n_row):
-            table = bins_refs[s][:rows, :]
-            tables = jnp.concatenate(
-                [jnp.where(table <= i.astype(jnp.float32).astype(jnp.bfloat16), one, zero) for i in ids], axis=1
-            )
-            part = lax.dot_general(
-                weights[:, s * rows : (s + 1) * rows],
-                tables,
-                (((1,), (0,)), ((), ())),
-                preferred_element_type=jnp.float32,
-            )
-            sums = part if sums is None else sums + part
+        table = wide_bins[...].astype(jnp.bfloat16)
+        tables = jnp.concatenate(
+            [jnp.where(table <= i.astype(jnp.float32).astype(jnp.bfloat16), one, zero) for i in ids], axis=1
+        )
+        sums = jnp.dot(weights[...], tables, preferred_element_type=jnp.float32)
         for j in range(steps):
             left = [sums[k * share : (k + 1) * share, j * width : (j + 1) * width] for k in range(17)]
             right = [totals[k] - left[k] for k in range(17)]
@@ -184,7 +177,10 @@
         ),
         in_specs=[vmem()] * (2 + n_row),
         out_specs=(vmem(), vmem()),
-        scratch_shapes=[pltpu.VMEM((-(-17 * share // 16) * 16, n_row * rows), jnp.bfloat16)],
+        scratch_shapes=[
+            pltpu.VMEM((-(-17 * share // 16) * 16, n_row * rows), jnp.bfloat16),
+            pltpu.VMEM((n_row * rows, width), jnp.float32),
+        ],
         compiler_params=pltpu.CompilerParams(vmem_limit_bytes=16 << 20),
         name="gains",
     )(values, jnp.tile(nbins, copies).reshape(1, width), *bins)

time: 41.5 us -> 38.4 us (0.925)
  Pallas kernels: 10.9 us -> 7.83 us
    pallas_call x1, Pallas kernels: 9.31 us -> 6.26 us  [split_gains(): pl.pallas_call(functools.partial(gain_kernel, n_row, share, features, STE...]
where the time goes in v1:
time: 38.4 us; the launch traced here: 38.3 us
  blocking collectives  12.9 us (34%)
  waiting for transfers between devices  11.1 us (29%)
  Pallas kernels  7.83 us (20%)
  starting transfers between devices  4.46 us (12%)
  local copies, waits for them, and re-layouts  1.05 us (3%)
  other arithmetic  0.93 us (2%)
    all_to_all x1, blocking collectives, on_device(): values = lax.all_to_all(copies, ('row', 'feat'), 0, 0)  12.9 us
    ppermute x4, waiting for transfers between devices, max_over(): lax.ppermute(x, axis, [(i, i ^ step) for i in range(size)])  11.1 us
    pallas_call x1, Pallas kernels, split_gains(): pl.pallas_call(functools.partial(gain_kernel, n_row, share, features, STE...  6.26 us
    ppermute x1, starting transfers between devices, on_device(): lax.ppermute(own, 'row', [((i + s) % n_row, i) for i in range(n_row)])  3.03 us
    pallas_call x1, Pallas kernels, prepare(): pl.pallas_call(prepare_kernel, out_shape=(jax.ShapeDtypeStruct((lines + t...  1.57 us
    ppermute x4, starting transfers between devices, max_over(): lax.ppermute(x, axis, [(i, i ^ step) for i in range(size)])  1.43 us
    div x1, other arithmetic, on_device(): return gain.reshape(share, features * BINS) / (best[:, :1] + epsilon)  0.8 us
  transfers between devices with their start and end apart: 5, of which 4 were waited for; matrix products, arithmetic and copies ran while one was open for 1% of the time, Pallas kernels for 0%

profile of v1, /device:TPU:0, one launch (start us, length us, event | category | flops | bytes accessed | tf_op | source)
XLA Modules:
  0.0 38.3 jit_solution(17547257989895584837)
XLA Ops:
  0.0 1.6 %prepare.1 = (bf16[1040,128]{1,0:T(8,128)(2,1)S(1)}, bf16[32,16,128]{2,1,0:T(8,128)(2,1)S(1)}) custom-call(s32[128,1024]{1,0:T(8,128)} %bins_hbm.1, s32[8,128]{1,0:T(8,128)} %bitcast.8, bf16[64,1000]{1,0:T(8,128)(2,1)} %logits_hbm.1, s32[1,64]{1,0:T(1,128)} %bitcast.9, bf16[16,1000]{1,0:T(8,128)(2,1)} %bitcast.7), custom_call_target="tpu_custom_call" | custom-call | tf_op jit(solution)/shard_map/prepare/pallas_call | solution.py:81
  1.6 3.0 %collective-permute-start = (bf16[1040,128]{1,0:T(8,128)(2,1)S(1)}, bf16[1040,128]{1,0:T(8,128)(2,1)S(1)}, u32[]{:S(2)}, u32[]{:S(2)}) collective-permute-start(bf16[1040,128]{1,0:T(8,128)(2,1)S(1)} %get-tuple-element.10.refs_0_), channel_id=1, source_target_pairs={{16,0},{0,16},{17,1},{1,17},{18,2},{2,18},{19,3},{3,19},{20,4},{4,... | collective-permute-start | bytes 798728 | tf_op jit(solution)/shard_map/ppermute | solution.py:202
  4.6 12.9 %all_to_all.5.values_ref = bf16[32,16,128]{2,1,0:T(8,128)(2,1)S(1)} all-to-all(bf16[32,16,128]{2,1,0:T(8,128)(2,1)S(1)} %get-tuple-element.9), channel_id=1, replica_groups=mesh['row'=2,'feat'=16] {'row','feat'}, dimensions={0} | all-to-all | bytes 262144 | tf_op jit(solution)/shard_map/all_to_all | solution.py:199
  17.5 0.0 copy-start
  17.5 0.0 collective-permute-done.refs_1_
  17.5 0.7 %copy-done = s32[128]{0:T(128)S(1)} copy-done((s32[128]{0:T(128)S(1)}, s32[128]{0:T(128)}, u32[]{:S(2)}) %copy-start) | copy-done | bytes 536
  18.2 6.3 %gains.1 = (f32[64,8,128]{2,1,0:T(8,128)S(1)}, f32[8,128]{1,0:T(8,128)S(1)}) custom-call(bf16[32,16,128]{2,1,0:T(8,128)(2,1)S(1)} %all_to_all.5.values_ref, s32[1,128]{1,0:T(1,128)S(1)} %bitcast.6, bf16[1040,128]{1,0:T(8,128)(2,1)S(1)} %get-tuple-element.10.refs_0_, bf16[1040,128]{1,0:T(8,128)(2,1)S(1)} %collective-permute-done.refs_1_), custom_call_target="tpu_custom_call" | custom-call | tf_op jit(solution)/shard_map/gains/pallas_call | solution.py:172
  24.5 0.3 collective-permute-start.1
  24.7 0.9 %collective-permute-done.1 = f32[8,128]{1,0:T(8,128)S(1)} collective-permute-done((f32[8,128]{1,0:T(8,128)S(1)}, f32[8,128]{1,0:T(8,128)S(1)}, u32[]{:S(2)}, u32[]{:S(2)}) %collective-permute-start.1) | collective-permute-done | bytes 4128 | tf_op jit(solution)/shard_map/ppermute | solution.py:192
  25.6 0.4 %collective-permute-start.2 = (f32[8,128]{1,0:T(8,128)S(1)}, f32[8,128]{1,0:T(8,128)S(1)}, u32[]{:S(2)}, u32[]{:S(2)}) collective-permute-start(f32[8,128]{1,0:T(8,128)S(1)} %max.12), channel_id=1, source_target_pairs={{0,2},{1,3},{2,0},{3,1},{4,6},{5,7},{6,4},{7,5},{8,10},{9,11},{10,... | collective-permute-start | bytes 12296 | tf_op jit(solution)/shard_map/ppermute | solution.py:192
  26.1 3.2 %collective-permute-done.2 = f32[8,128]{1,0:T(8,128)S(1)} collective-permute-done((f32[8,128]{1,0:T(8,128)S(1)}, f32[8,128]{1,0:T(8,128)S(1)}, u32[]{:S(2)}, u32[]{:S(2)}) %collective-permute-start.2) | collective-permute-done | bytes 4128 | tf_op jit(solution)/shard_map/ppermute | solution.py:192
  29.2 0.0 collective-permute-start.3
  29.3 3.6 %collective-permute-done.3 = f32[8,128]{1,0:T(8,128)S(1)} collective-permute-done((f32[8,128]{1,0:T(8,128)S(1)}, f32[8,128]{1,0:T(8,128)S(1)}, u32[]{:S(2)}, u32[]{:S(2)}) %collective-permute-start.3) | collective-permute-done | bytes 4128 | tf_op jit(solution)/shard_map/ppermute | solution.py:192
  32.9 0.7 %collective-permute-start.4 = (f32[8,128]{1,0:T(8,128)S(1)}, f32[8,128]{1,0:T(8,128)S(1)}, u32[]{:S(2)}, u32[]{:S(2)}) collective-permute-start(f32[8,128]{1,0:T(8,128)S(1)} %max.14), channel_id=1, source_target_pairs={{0,8},{1,9},{2,10},{3,11},{4,12},{5,13},{6,14},{7,15},{8,0},{9,1},... | collective-permute-start | bytes 12296 | tf_op jit(solution)/shard_map/ppermute | solution.py:192
  33.6 0.2 copy.7
  33.8 0.2 reshape.11
  34.0 3.4 %collective-permute-done.4 = f32[8,128]{1,0:T(8,128)S(1)} collective-permute-done((f32[8,128]{1,0:T(8,128)S(1)}, f32[8,128]{1,0:T(8,128)S(1)}, u32[]{:S(2)}, u32[]{:S(2)}) %collective-permute-start.4) | collective-permute-done | bytes 4128 | tf_op jit(solution)/shard_map/ppermute | solution.py:192
  37.4 0.1 add_reduce_fusion
  37.5 0.8 %broadcast_divide_fusion = f32[8,8192]{1,0:T(8,128)} fusion(f32[8,8192]{1,0:T(8,128)S(1)} %reshape.11, f32[8]{0:T(128)S(1)} %add_reduce_fusion), kind=kLoop, calls=%fused_computation | loop fusion | flops 65536 | bytes 524320 | tf_op jit(solution)/shard_map/div | solution.py:207
  (4 shorter events, 0.0 us)
Async XLA Ops:
  1.6 16.0 %collective-permute-start = (bf16[1040,128]{1,0:T(8,128)(2,1)S(1)}, bf16[1040,128]{1,0:T(8,128)(2,1)S(1)}, u32[]{:S(2)}, u32[]{:S(2)}) collective-permute-start(bf16[1040,128]{1,0:T(8,128)(2,1)S(1)} %get-tuple-element.10.refs_0_), channel_id=1, source_target_pairs={{16,0},{0,16},{17,1},{1,17},{18,2},{2,18},{19,3},{3,19},{20,4},{4,... | collective-permute-start | bytes 798728 | tf_op jit(solution)/shard_map/ppermute | solution.py:202
  17.5 0.7 %copy-start = (s32[128]{0:T(128)S(1)}, s32[128]{0:T(128)}, u32[]{:S(2)}) copy-start(s32[128]{0:T(128)} %param.10) | copy-start | bytes 1540
  24.5 1.2 %collective-permute-start.1 = (f32[8,128]{1,0:T(8,128)S(1)}, f32[8,128]{1,0:T(8,128)S(1)}, u32[]{:S(2)}, u32[]{:S(2)}) collective-permute-start(f32[8,128]{1,0:T(8,128)S(1)} %get-tuple-element.12), channel_id=1, source_target_pairs={{0,1},{1,0},{2,3},{3,2},{4,5},{5,4},{6,7},{7,6},{8,9},{9,8},{10,11... | collective-permute-start | bytes 12296 | tf_op jit(solution)/shard_map/ppermute | solution.py:192
  25.6 3.6 %collective-permute-start.2 = (f32[8,128]{1,0:T(8,128)S(1)}, f32[8,128]{1,0:T(8,128)S(1)}, u32[]{:S(2)}, u32[]{:S(2)}) collective-permute-start(f32[8,128]{1,0:T(8,128)S(1)} %max.12), channel_id=1, source_target_pairs={{0,2},{1,3},{2,0},{3,1},{4,6},{5,7},{6,4},{7,5},{8,10},{9,11},{10,... | collective-permute-start | bytes 12296 | tf_op jit(solution)/shard_map/ppermute | solution.py:192
  29.2 3.6 %collective-permute-start.3 = (f32[8,128]{1,0:T(8,128)S(1)}, f32[8,128]{1,0:T(8,128)S(1)}, u32[]{:S(2)}, u32[]{:S(2)}) collective-permute-start(f32[8,128]{1,0:T(8,128)S(1)} %max.13), channel_id=1, source_target_pairs={{0,4},{1,5},{2,6},{3,7},{4,0},{5,1},{6,2},{7,3},{8,12},{9,13},{10,... | collective-permute-start | bytes 12296 | tf_op jit(solution)/shard_map/ppermute | solution.py:192
  32.9 4.5 %collective-permute-start.4 = (f32[8,128]{1,0:T(8,128)S(1)}, f32[8,128]{1,0:T(8,128)S(1)}, u32[]{:S(2)}, u32[]{:S(2)}) collective-permute-start(f32[8,128]{1,0:T(8,128)S(1)} %max.14), channel_id=1, source_target_pairs={{0,8},{1,9},{2,10},{3,11},{4,12},{5,13},{6,14},{7,15},{8,0},{9,1},... | collective-permute-start | bytes 12296 | tf_op jit(solution)/shard_map/ppermute | solution.py:192

commit v2 on v1

v2 whole, which is shorter than its diff:
```python
import functools

import jax
import jax.numpy as jnp
from jax import lax
from jax.experimental import pallas as pl
from jax.experimental.pallas import tpu as pltpu
from jax.sharding import PartitionSpec as P


BINS = 64
LEAVES = 16
LANES = 128
STEPS = 16
ridge = 1.0
epsilon = 1e-06


def vmem():
    return pl.BlockSpec(memory_space=pltpu.VMEM)


def lanes_of(features):
    return features * max(1, LANES // features)


def prepare_kernel(*refs):
    bins_hbm, leaf_hbm, logits_hbm, labels_hbm, projection_hbm, nbins_hbm, turned_ref, values_ref, nbins_ref = refs[:9]
    bins_ref, leaf_ref, logits_ref, labels_ref, projection_ref, arrived = refs[9:]
    pairs = (
        (logits_hbm, logits_ref),
        (labels_hbm, labels_ref),
        (projection_hbm, projection_ref),
        (bins_hbm, bins_ref),
        (leaf_hbm, leaf_ref),
        (nbins_hbm, nbins_ref),
    )
    arrivals = [pltpu.make_async_copy(a, b, arrived.at[i]) for i, (a, b) in enumerate(pairs)]
    for arrival in arrivals:
        arrival.start()
    for arrival in arrivals[:3]:
        arrival.wait()

    rows, classes = logits_ref.shape
    scores = logits_ref[...].astype(jnp.float32)
    highest = jnp.max(scores, axis=1, keepdims=True)
    expd = jnp.exp(scores - highest)
    probability = expd / jnp.sum(expd, axis=1, keepdims=True)
    labels = jnp.broadcast_to(labels_ref[...].astype(jnp.float32), (LANES, rows))
    labels = jnp.transpose(labels)[:, :1].astype(jnp.int32)
    lane = lax.broadcasted_iota(jnp.int32, (rows, classes), 1)
    target = jnp.where(lane == labels, 1.0, 0.0)
    gradient = (probability - target).astype(jnp.bfloat16)
    sketch = lax.dot_general(
        projection_ref[...], gradient, (((1,), (1,)), ((), ())), preferred_element_type=jnp.float32
    )
    hessian = jnp.sum(probability * (1.0 - probability), axis=1, keepdims=True)
    hessian = jnp.transpose(jnp.broadcast_to(hessian, (rows, LANES)))[:1, :]
    top = sketch[:10]
    low = jnp.concatenate([sketch[10:], hessian, jnp.zeros((3, rows), jnp.float32)], axis=0)
    packed = jnp.concatenate([top, low], axis=1)
    odd = lax.rem(lax.axis_index("feat"), 2)
    packed = jnp.where(odd == 1, pltpu.roll(packed, rows, 1), packed).astype(jnp.bfloat16)
    for c in range(5):
        block = packed[2 * c : 2 * c + 2]
        cols = slice(c * LANES, (c + 1) * LANES)
        values_ref[:, :, cols] = jnp.broadcast_to(block[None], (values_ref.shape[0], 2, LANES))

    for arrival in arrivals[3:]:
        arrival.wait()
    lines = bins_ref.shape[1]
    turned = jnp.transpose(bins_ref[...].astype(jnp.float32))
    copies = turned_ref.shape[1] // bins_ref.shape[0]
    if copies > 1:
        turned = jnp.concatenate([turned] * copies, axis=1)
    turned_ref[:lines, :] = turned.astype(jnp.bfloat16)
    leaf = leaf_ref[...].astype(jnp.float32)
    spare = turned_ref.shape[0] - lines - leaf.shape[0]
    leaf = jnp.concatenate([leaf, jnp.zeros((spare, LANES), jnp.float32)], axis=0) if spare else leaf
    turned_ref[lines:, :LANES] = leaf.astype(jnp.bfloat16)


def prepare(bins, leaf, logits, labels, projection, nbins, destinations):
    features, lines = bins.shape
    rows = logits.shape[0]
    tail = -(-lines // LANES // 16) * 16
    width = lanes_of(features)
    counts = jnp.tile(nbins, width // features).reshape(1, width)
    given = (bins, leaf.reshape(lines // LANES, LANES), logits, labels.reshape(1, rows), projection.T, counts)
    return pl.pallas_call(
        prepare_kernel,
        out_shape=(
            jax.ShapeDtypeStruct((lines + tail, lanes_of(features)), jnp.bfloat16),
            jax.ShapeDtypeStruct((destinations, 2, 10 * rows), jnp.bfloat16),
            jax.ShapeDtypeStruct((1, width), jnp.int32),
        ),
        in_specs=[pl.BlockSpec(memory_space=pltpu.HBM)] * 6,
        out_specs=(vmem(), vmem(), vmem()),
        scratch_shapes=[pltpu.VMEM(x.shape, x.dtype) for x in given[:5]] + [pltpu.SemaphoreType.DMA((6,))],
        compiler_params=pltpu.CompilerParams(vmem_limit_bytes=16 << 20),
        name="prepare",
    )(*[pltpu.with_memory_space_constraint(x, pltpu.HBM) for x in given])


def padded(share):
    return -(-17 * share // 16) * 16


def fill_weights(share, shard, values_ref, bins_ref, weights, table):
    sources, half = values_ref.shape[0] // lax.axis_size("row"), LANES // 2
    rows = sources * half
    wide = (share, LANES)
    my_leaf = lax.broadcasted_iota(jnp.int32, wide, 0) + lax.axis_index("row") * share
    my_leaf = my_leaf.astype(jnp.float32)
    left_half = lax.broadcasted_iota(jnp.int32, (2, LANES), 1) < half
    totals = [jnp.zeros(wide, jnp.float32) for _ in range(17)]
    for pair in range(sources // 2):
        columns = [None] * 20
        for c in range(5):
            cols = slice(c * LANES, (c + 1) * LANES)
            first = values_ref[shard * sources + 2 * pair, :, cols].astype(jnp.float32)
            second = values_ref[shard * sources + 2 * pair + 1, :, cols].astype(jnp.float32)
            top = jnp.where(left_half, first, second)
            low = pltpu.roll(jnp.where(left_half, second, first), half, 1)
            columns[2 * c : 2 * c + 2] = top[:1], top[1:]
            columns[10 + 2 * c : 12 + 2 * c] = low[:1], low[1:]
        at = rows + pair // 16 * 16
        leaf = bins_ref[at : at + 16, :LANES].astype(jnp.float32)[pair % 16 : pair % 16 + 1]
        mine = jnp.broadcast_to(leaf, wide) == my_leaf
        pieces = []
        for k in range(17):
            piece = jnp.where(mine, jnp.broadcast_to(columns[k], wide), 0.0)
            totals[k] = totals[k] + piece
            pieces.append(piece)
        spare = padded(share) - 17 * share
        if spare:
            pieces.append(jnp.zeros((spare, LANES), jnp.float32))
        lines = jnp.concatenate(pieces, axis=0).astype(jnp.bfloat16)
        weights[:, pair * LANES : (pair + 1) * LANES] = lines
    table[...] = bins_ref[:rows, :].astype(jnp.float32)
    return totals


def left_sums(ids, weights, table):
    one, zero = jnp.bfloat16(1.0), jnp.bfloat16(0.0)
    bins = table[...].astype(jnp.bfloat16)
    ids = [i.astype(jnp.float32).astype(jnp.bfloat16) for i in ids]
    tables = jnp.concatenate([jnp.where(bins <= i, one, zero) for i in ids], axis=1)
    return jnp.dot(weights[...], tables, preferred_element_type=jnp.float32)


def sums_kernel(share, features, steps, shift, values_ref, bins_ref, *refs):
    n_row = lax.axis_size("row")
    earlier, (sums_ref, totals_ref, weights, table) = refs[:-4], refs[-4:]
    shard = lax.rem(lax.axis_index("row") + shift, n_row)
    totals = fill_weights(share, shard, values_ref, bins_ref, weights, table)
    for k in range(17):
        totals_ref[k] = totals[k] + earlier[1][k] if earlier else totals[k]
    width = bins_ref.shape[1]
    copies = width // features
    bin_of = lax.broadcasted_iota(jnp.int32, (1, width), 1) // features

    def add_group(g, carry):
        ids = [bin_of + (g * steps + j) * copies for j in range(steps)]
        sums = left_sums(ids, weights, table)
        for j in range(steps):
            part = sums[: 17 * share, j * width : (j + 1) * width]
            sums_ref[g * steps + j] = part + earlier[0][g * steps + j] if earlier else part
        return carry

    lax.fori_loop(0, BINS // copies // steps, add_group, 0)


def partial_sums(values, bins, share, features, shift, earlier):
    width = bins.shape[1]
    rows = values.shape[0] // lax.axis_size("row") * LANES // 2
    return pl.pallas_call(
        functools.partial(sums_kernel, share, features, STEPS, shift),
        out_shape=(
            jax.ShapeDtypeStruct((BINS * features // width, 17 * share, width), jnp.float32),
            jax.ShapeDtypeStruct((17, share, LANES), jnp.float32),
        ),
        in_specs=[vmem()] * (2 + len(earlier)),
        out_specs=(vmem(), vmem()),
        scratch_shapes=[
            pltpu.VMEM((padded(share), rows), jnp.bfloat16),
            pltpu.VMEM((rows, width), jnp.float32),
        ],
        compiler_params=pltpu.CompilerParams(vmem_limit_bytes=16 << 20),
        name="sums",
    )(values, bins, *earlier)


def gain_kernel(share, features, steps, shift, values_ref, nbins_ref, bins_ref, *refs):
    n_row = lax.axis_size("row")
    earlier, (gain_ref, best_ref, weights, table) = refs[:-4], refs[-4:]
    shard = lax.rem(lax.axis_index("row") + shift, n_row)
    totals = fill_weights(share, shard, values_ref, bins_ref, weights, table)
    width = bins_ref.shape[1]
    full = (share, width)
    if earlier:
        totals = [t + earlier[1][k] for k, t in enumerate(totals)]
    totals = [jnp.broadcast_to(jnp.sum(t, axis=1, keepdims=True), full) for t in totals]

    def score(sums):
        squares = sums[0] * sums[0]
        for k in range(1, 16):
            squares = squares + sums[k] * sums[k]
        return squares / (sums[16] + ridge)

    of_all = score(totals)
    copies = width // features
    bin_of = lax.broadcasted_iota(jnp.int32, (1, width), 1) // features
    last = jnp.broadcast_to(nbins_ref[...] - 1, full)

    def add_group(g, best):
        ids = [bin_of + (g * steps + j) * copies for j in range(steps)]
        sums = left_sums(ids, weights, table)
        for j in range(steps):
            left = [sums[k * share : (k + 1) * share, j * width : (j + 1) * width] for k in range(17)]
            if earlier:
                left = [s + earlier[0][g * steps + j, k * share : (k + 1) * share] for k, s in enumerate(left)]
            right = [totals[k] - left[k] for k in range(17)]
            gain = score(left) + score(right) - of_all
            gain = jnp.where(jnp.broadcast_to(ids[j], full) < last, gain, 0.0)
            gain_ref[g * steps + j] = gain
            best = jnp.maximum(best, gain)
        return best

    count = BINS // copies // steps
    best = lax.fori_loop(0, count, add_group, jnp.full(full, -jnp.inf, jnp.float32))
    best = jnp.broadcast_to(jnp.max(best, axis=1, keepdims=True), (share, LANES))
    mine = lax.broadcasted_iota(jnp.int32, (share, LANES), 0) == lax.broadcasted_iota(jnp.int32, (share, LANES), 1)
    best_ref[...] = jnp.max(jnp.where(mine, best, -jnp.inf), axis=0, keepdims=True)


def split_gains(values, counts, bins, share, features, shift, earlier):
    width = bins.shape[1]
    copies = width // features
    rows = values.shape[0] // lax.axis_size("row") * LANES // 2
    return pl.pallas_call(
        functools.partial(gain_kernel, share, features, STEPS, shift),
        out_shape=(
            jax.ShapeDtypeStruct((BINS // copies, share, width), jnp.float32),
            jax.ShapeDtypeStruct((1, LANES), jnp.float32),
        ),
        in_specs=[vmem()] * (3 + len(earlier)),
        out_specs=(vmem(), vmem()),
        scratch_shapes=[
            pltpu.VMEM((padded(share), rows), jnp.bfloat16),
            pltpu.VMEM((rows, width), jnp.float32),
        ],
        compiler_params=pltpu.CompilerParams(vmem_limit_bytes=16 << 20),
        name="gains",
    )(values, counts, bins, *earlier)


def max_over(x, axis, size):
    step = 1
    while step < size:
        x = jnp.maximum(x, lax.ppermute(x, axis, [(i, i ^ step) for i in range(size)]))
        step *= 2
    return x


def on_device(n_row, n_feat, logits, labels, projection, bins, nbins, leaf):
    own, copies, counts = prepare(bins, leaf, logits, labels, projection, nbins, n_row * n_feat)
    values = lax.all_to_all(copies, ("row", "feat"), 0, 0)
    all_bins = [own]
    for s in range(1, n_row):
        all_bins.append(lax.ppermute(own, "row", [((i + s) % n_row, i) for i in range(n_row)]))
    share, features = LEAVES // n_row, bins.shape[0]
    earlier = ()
    for s in range(n_row - 1):
        earlier = partial_sums(values, all_bins[s], share, features, s, earlier)
    gain, best = split_gains(values, counts, all_bins[-1], share, features, n_row - 1, earlier)
    best = max_over(best, "feat", n_feat)
    gain = gain.transpose(1, 0, 2).reshape(share, BINS, features).transpose(0, 2, 1)
    return gain.reshape(share, features * BINS) / (best[0, :share, None] + epsilon)


def solution(mesh):
    return jax.shard_map(
        functools.partial(on_device, mesh.shape["row"], mesh.shape["feat"]),
        mesh=mesh,
        in_specs=(
            P(("row", "feat"), None),
            P(("row", "feat")),
            P(),
            P("feat", "row"),
            P("feat"),
            P("row"),
        ),
        out_specs=P("row", "feat"),
        check_vma=False,
    )
```

time: 38.4 us -> 38 us (0.990)
  Pallas kernels: 7.83 us -> 8.87 us
  local copies, waits for them, and re-layouts: 1.05 us -> 0.4 us
  blocking collectives: 12.9 us -> 12.3 us
    pallas_call x1 -> x2, Pallas kernels: 6.26 us -> 7.18 us  [the longest x1 3.82 us: split_gains(): pl.pallas_call(functools.partial(gain_kernel, share, features, STEPS, shi...]
    unnamed x2 -> x0, local copies, waits for them, and re-layouts: 0.65 us -> none
    all_to_all x1, blocking collectives: 12.9 us -> 12.3 us  [on_device(): values = lax.all_to_all(copies, ('row', 'feat'), 0, 0)]
  transfers between devices with their start and end apart: 5 -> 5, of which waited for: 4 -> 4; matrix products, arithmetic and copies ran while one was open for 1% -> 1% of each run, Pallas kernels for 0% -> 9%
where the time goes in v2:
time: 38 us; the launch traced here: 37.8 us
  blocking collectives  12.3 us (32%)
  waiting for transfers between devices  10.9 us (29%)
  Pallas kernels  8.87 us (23%)
  starting transfers between devices  4.48 us (12%)
  other arithmetic  0.82 us (2%)
  local copies, waits for them, and re-layouts  0.4 us (1%)
    all_to_all x1, blocking collectives, on_device(): values = lax.all_to_all(copies, ('row', 'feat'), 0, 0)  12.3 us
    ppermute x4, waiting for transfers between devices, max_over(): lax.ppermute(x, axis, [(i, i ^ step) for i in range(size)])  10.9 us
    pallas_call x1, Pallas kernels, split_gains(): pl.pallas_call(functools.partial(gain_kernel, share, features, STEPS, shi...  3.82 us
    pallas_call x1, Pallas kernels, partial_sums(): pl.pallas_call(functools.partial(sums_kernel, share, features, STEPS, shi...  3.36 us
    ppermute x1, starting transfers between devices, on_device(): lax.ppermute(own, 'row', [((i + s) % n_row, i) for i in range(n_row)])  3.03 us
    pallas_call x1, Pallas kernels, prepare(): pl.pallas_call(prepare_kernel, out_shape=(jax.ShapeDtypeStruct((lines + t...  1.69 us
    ppermute x4, starting transfers between devices, max_over(): lax.ppermute(x, axis, [(i, i ^ step) for i in range(size)])  1.45 us
    div x1, other arithmetic, on_device(): gain.reshape(share, features * BINS) / (best[0, :share, None] + epsilon)  0.8 us
  transfers between devices with their start and end apart: 5, of which 4 were waited for; matrix products, arithmetic and copies ran while one was open for 1% of the time, Pallas kernels for 9%

profile of v2, /device:TPU:0, one launch (start us, length us, event | category | flops | bytes accessed | tf_op | source)
XLA Modules:
  0.0 37.8 jit_solution(4580698309281443571)
XLA Ops:
  0.0 1.7 %prepare.1 = (bf16[1040,128]{1,0:T(8,128)(2,1)S(1)}, bf16[32,2,640]{2,1,0:T(2,128)(2,1)S(1)}, s32[1,128]{1,0:T(1,128)S(1)}) custom-call(s32[128,1024]{1,0:T(8,128)} %refs_0_.1, s32[8,128]{1,0:T(8,128)} %bitcast.9, bf16[64,1000]{1,0:T(8,128)(2,1)} %refs_2_.1, s32[1,64]{1,0:T(1,128)} %bitcast.10, bf16[16,1000]{1,0:T(8,128)(2,1)} %bitcast.8, s32[1,128]{1,0:T(1,128)} %bitcast.11), custom_call_target="tpu_custom_call" | custom-call | tf_op jit(solution)/shard_map/prepare/pallas_call | solution.py:90
  1.7 3.0 %collective-permute-start = (bf16[1040,128]{1,0:T(8,128)(2,1)S(1)}, bf16[1040,128]{1,0:T(8,128)(2,1)S(1)}, u32[]{:S(2)}, u32[]{:S(2)}) collective-permute-start(bf16[1040,128]{1,0:T(8,128)(2,1)S(1)} %get-tuple-element.14.bins_ref), channel_id=1, source_target_pairs={{16,0},{0,16},{17,1},{1,17},{18,2},{2,18},{19,3},{3,19},{20,4},{4,... | collective-permute-start | bytes 798728 | tf_op jit(solution)/shard_map/ppermute | solution.py:271
  4.7 12.3 %all_to_all.5.values_ref = bf16[32,2,640]{2,1,0:T(2,128)(2,1)S(1)} all-to-all(bf16[32,2,640]{2,1,0:T(2,128)(2,1)S(1)} %get-tuple-element.12), channel_id=1, replica_groups=mesh['row'=2,'feat'=16] {'row','feat'}, dimensions={0} | all-to-all | bytes 163840 | tf_op jit(solution)/shard_map/all_to_all | solution.py:268
  17.0 3.4 %sums.1 = (f32[64,136,128]{2,1,0:T(8,128)S(1)}, f32[17,8,128]{2,1,0:T(8,128)S(1)}) custom-call(bf16[32,2,640]{2,1,0:T(2,128)(2,1)S(1)} %all_to_all.5.values_ref, bf16[1040,128]{1,0:T(8,128)(2,1)S(1)} %get-tuple-element.14.bins_ref), custom_call_target="tpu_custom_call" | custom-call | tf_op jit(solution)/shard_map/sums/pallas_call | solution.py:177
  20.4 0.0 collective-permute-done.bins_ref
  20.4 3.8 %gains.1 = (f32[64,8,128]{2,1,0:T(8,128)S(1)}, f32[1,128]{1,0:T(1,128)S(1)}) custom-call(bf16[32,2,640]{2,1,0:T(2,128)(2,1)S(1)} %all_to_all.5.values_ref, s32[1,128]{1,0:T(1,128)S(1)} %get-tuple-element.13.nbins_ref, bf16[1040,128]{1,0:T(8,128)(2,1)S(1)} %collective-permute-done.bins_ref, f32[64,136,128]{2,1,0:T(8,128)S(1)} %get-tuple-element.15.refs_0_, ...), custom_call_target="tpu_custom_call" | custom-call | tf_op jit(solution)/shard_map/gains/pallas_call | solution.py:241
  24.2 0.1 collective-permute-start.1
  24.3 1.0 %collective-permute-done.1 = f32[1,128]{1,0:T(1,128)S(1)} collective-permute-done((f32[1,128]{1,0:T(1,128)S(1)}, f32[1,128]{1,0:T(1,128)S(1)}, u32[]{:S(2)}, u32[]{:S(2)}) %collective-permute-start.1) | collective-permute-done | bytes 544 | tf_op jit(solution)/shard_map/ppermute | solution.py:261
  25.4 0.4 %collective-permute-start.2 = (f32[1,128]{1,0:T(1,128)S(1)}, f32[1,128]{1,0:T(1,128)S(1)}, u32[]{:S(2)}, u32[]{:S(2)}) collective-permute-start(f32[1,128]{1,0:T(1,128)S(1)} %max.12), channel_id=1, source_target_pairs={{0,2},{1,3},{2,0},{3,1},{4,6},{5,7},{6,4},{7,5},{8,10},{9,11},{10,... | collective-permute-start | bytes 1544 | tf_op jit(solution)/shard_map/ppermute | solution.py:261
  25.8 3.1 %collective-permute-done.2 = f32[1,128]{1,0:T(1,128)S(1)} collective-permute-done((f32[1,128]{1,0:T(1,128)S(1)}, f32[1,128]{1,0:T(1,128)S(1)}, u32[]{:S(2)}, u32[]{:S(2)}) %collective-permute-start.2) | collective-permute-done | bytes 544 | tf_op jit(solution)/shard_map/ppermute | solution.py:261
  29.0 0.3 collective-permute-start.3
  29.3 3.3 %collective-permute-done.3 = f32[1,128]{1,0:T(1,128)S(1)} collective-permute-done((f32[1,128]{1,0:T(1,128)S(1)}, f32[1,128]{1,0:T(1,128)S(1)}, u32[]{:S(2)}, u32[]{:S(2)}) %collective-permute-start.3) | collective-permute-done | bytes 544 | tf_op jit(solution)/shard_map/ppermute | solution.py:261
  32.5 0.6 %collective-permute-start.4 = (f32[1,128]{1,0:T(1,128)S(1)}, f32[1,128]{1,0:T(1,128)S(1)}, u32[]{:S(2)}, u32[]{:S(2)}) collective-permute-start(f32[1,128]{1,0:T(1,128)S(1)} %max.14), channel_id=1, source_target_pairs={{0,8},{1,9},{2,10},{3,11},{4,12},{5,13},{6,14},{7,15},{8,0},{9,1},... | collective-permute-start | bytes 1544 | tf_op jit(solution)/shard_map/ppermute | solution.py:261
  33.2 0.2 copy.7
  33.4 0.2 reshape.20
  33.6 3.4 %collective-permute-done.4 = f32[1,128]{1,0:T(1,128)S(1)} collective-permute-done((f32[1,128]{1,0:T(1,128)S(1)}, f32[1,128]{1,0:T(1,128)S(1)}, u32[]{:S(2)}, u32[]{:S(2)}) %collective-permute-start.4) | collective-permute-done | bytes 544 | tf_op jit(solution)/shard_map/ppermute | solution.py:261
  37.0 0.8 %broadcast_divide_fusion = f32[8,8192]{1,0:T(8,128)} fusion(f32[8,8192]{1,0:T(8,128)S(1)} %reshape.20, f32[8]{0:T(128)S(1)} %add_bitcast_fusion), kind=kLoop, calls=%fused_computation | loop fusion | flops 65536 | bytes 524320 | tf_op jit(solution)/shard_map/div | solution.py:279
  (5 shorter events, 0.0 us)
Async XLA Ops:
  1.7 18.7 %collective-permute-start = (bf16[1040,128]{1,0:T(8,128)(2,1)S(1)}, bf16[1040,128]{1,0:T(8,128)(2,1)S(1)}, u32[]{:S(2)}, u32[]{:S(2)}) collective-permute-start(bf16[1040,128]{1,0:T(8,128)(2,1)S(1)} %get-tuple-element.14.bins_ref), channel_id=1, source_target_pairs={{16,0},{0,16},{17,1},{1,17},{18,2},{2,18},{19,3},{3,19},{20,4},{4,... | collective-permute-start | bytes 798728 | tf_op jit(solution)/shard_map/ppermute | solution.py:271
  24.2 1.2 %collective-permute-start.1 = (f32[1,128]{1,0:T(1,128)S(1)}, f32[1,128]{1,0:T(1,128)S(1)}, u32[]{:S(2)}, u32[]{:S(2)}) collective-permute-start(f32[1,128]{1,0:T(1,128)S(1)} %get-tuple-element.18), channel_id=1, source_target_pairs={{0,1},{1,0},{2,3},{3,2},{4,5},{5,4},{6,7},{7,6},{8,9},{9,8},{10,11... | collective-permute-start | bytes 1544 | tf_op jit(solution)/shard_map/ppermute | solution.py:261
  25.4 3.6 %collective-permute-start.2 = (f32[1,128]{1,0:T(1,128)S(1)}, f32[1,128]{1,0:T(1,128)S(1)}, u32[]{:S(2)}, u32[]{:S(2)}) collective-permute-start(f32[1,128]{1,0:T(1,128)S(1)} %max.12), channel_id=1, source_target_pairs={{0,2},{1,3},{2,0},{3,1},{4,6},{5,7},{6,4},{7,5},{8,10},{9,11},{10,... | collective-permute-start | bytes 1544 | tf_op jit(solution)/shard_map/ppermute | solution.py:261
  29.0 3.6 %collective-permute-start.3 = (f32[1,128]{1,0:T(1,128)S(1)}, f32[1,128]{1,0:T(1,128)S(1)}, u32[]{:S(2)}, u32[]{:S(2)}) collective-permute-start(f32[1,128]{1,0:T(1,128)S(1)} %max.13), channel_id=1, source_target_pairs={{0,4},{1,5},{2,6},{3,7},{4,0},{5,1},{6,2},{7,3},{8,12},{9,13},{10,... | collective-permute-start | bytes 1544 | tf_op jit(solution)/shard_map/ppermute | solution.py:261
  32.5 4.5 %collective-permute-start.4 = (f32[1,128]{1,0:T(1,128)S(1)}, f32[1,128]{1,0:T(1,128)S(1)}, u32[]{:S(2)}, u32[]{:S(2)}) collective-permute-start(f32[1,128]{1,0:T(1,128)S(1)} %max.14), channel_id=1, source_target_pairs={{0,8},{1,9},{2,10},{3,11},{4,12},{5,13},{6,14},{7,15},{8,0},{9,1},... | collective-permute-start | bytes 1544 | tf_op jit(solution)/shard_map/ppermute | solution.py:261

commit v3 on v2

--- a/solution.py
+++ b/solution.py
@@ -11,7 +11,7 @@
 BINS = 64
 LEAVES = 16
 LANES = 128
-STEPS = 16
+STEPS = 64
 ridge = 1.0
 epsilon = 1e-06
 
@@ -175,7 +175,7 @@
     width = bins.shape[1]
     rows = values.shape[0] // lax.axis_size("row") * LANES // 2
     return pl.pallas_call(
-        functools.partial(sums_kernel, share, features, STEPS, shift),
+        functools.partial(sums_kernel, share, features, min(STEPS, BINS * features // width), shift),
         out_shape=(
             jax.ShapeDtypeStruct((BINS * features // width, 17 * share, width), jnp.float32),
             jax.ShapeDtypeStruct((17, share, LANES), jnp.float32),
@@ -239,7 +239,7 @@
     copies = width // features
     rows = values.shape[0] // lax.axis_size("row") * LANES // 2
     return pl.pallas_call(
-        functools.partial(gain_kernel, share, features, STEPS, shift),
+        functools.partial(gain_kernel, share, features, min(STEPS, BINS // copies), shift),
         out_shape=(
             jax.ShapeDtypeStruct((BINS // copies, share, width), jnp.float32),
             jax.ShapeDtypeStruct((1, LANES), jnp.float32),

time: 38 us -> 36.6 us (0.963)
  Pallas kernels: 8.87 us -> 7.52 us
    pallas_call x2, Pallas kernels: 7.18 us -> 5.83 us  [the longest x1 3.13 us: split_gains(): pl.pallas_call(functools.partial(gain_kernel, share, features, min(STEPS,...]
  transfers between devices with their start and end apart: 5 -> 5, of which waited for: 4 -> 4; matrix products, arithmetic and copies ran while one was open for 1% -> 1% of each run, Pallas kernels for 9% -> 7%
where the time goes in v3:
time: 36.6 us; the launch traced here: 36.5 us
  blocking collectives  12.3 us (34%)
  waiting for transfers between devices  10.9 us (30%)
  Pallas kernels  7.52 us (21%)
  starting transfers between devices  4.49 us (12%)
  other arithmetic  0.82 us (2%)
  local copies, waits for them, and re-layouts  0.4 us (1%)
    all_to_all x1, blocking collectives, on_device(): values = lax.all_to_all(copies, ('row', 'feat'), 0, 0)  12.3 us
    ppermute x4, waiting for transfers between devices, max_over(): lax.ppermute(x, axis, [(i, i ^ step) for i in range(size)])  10.9 us
    pallas_call x1, Pallas kernels, split_gains(): pl.pallas_call(functools.partial(gain_kernel, share, features, min(STEPS,...  3.13 us
    ppermute x1, starting transfers between devices, on_device(): lax.ppermute(own, 'row', [((i + s) % n_row, i) for i in range(n_row)])  3.03 us
    pallas_call x1, Pallas kernels, partial_sums(): pl.pallas_call(functools.partial(sums_kernel, share, features, min(STEPS,...  2.7 us
    pallas_call x1, Pallas kernels, prepare(): pl.pallas_call(prepare_kernel, out_shape=(jax.ShapeDtypeStruct((lines + t...  1.69 us
    ppermute x4, starting transfers between devices, max_over(): lax.ppermute(x, axis, [(i, i ^ step) for i in range(size)])  1.46 us
    div x1, other arithmetic, on_device(): gain.reshape(share, features * BINS) / (best[0, :share, None] + epsilon)  0.8 us
  transfers between devices with their start and end apart: 5, of which 4 were waited for; matrix products, arithmetic and copies ran while one was open for 1% of the time, Pallas kernels for 7%

profile of v3, /device:TPU:0, one launch (start us, length us, event | category | flops | bytes accessed | tf_op | source)
XLA Modules:
  0.0 36.5 jit_solution(11487967453557472322)
XLA Ops:
  0.0 1.7 %prepare.1 = (bf16[1040,128]{1,0:T(8,128)(2,1)S(1)}, bf16[32,2,640]{2,1,0:T(2,128)(2,1)S(1)}, s32[1,128]{1,0:T(1,128)S(1)}) custom-call(s32[128,1024]{1,0:T(8,128)} %refs_0_.1, s32[8,128]{1,0:T(8,128)} %bitcast.9, bf16[64,1000]{1,0:T(8,128)(2,1)} %refs_2_.1, s32[1,64]{1,0:T(1,128)} %bitcast.10, bf16[16,1000]{1,0:T(8,128)(2,1)} %bitcast.8, s32[1,128]{1,0:T(1,128)} %bitcast.11), custom_call_target="tpu_custom_call" | custom-call | tf_op jit(solution)/shard_map/prepare/pallas_call | solution.py:90
  1.7 3.0 %collective-permute-start = (bf16[1040,128]{1,0:T(8,128)(2,1)S(1)}, bf16[1040,128]{1,0:T(8,128)(2,1)S(1)}, u32[]{:S(2)}, u32[]{:S(2)}) collective-permute-start(bf16[1040,128]{1,0:T(8,128)(2,1)S(1)} %get-tuple-element.14.bins_ref), channel_id=1, source_target_pairs={{16,0},{0,16},{17,1},{1,17},{18,2},{2,18},{19,3},{3,19},{20,4},{4,... | collective-permute-start | bytes 798728 | tf_op jit(solution)/shard_map/ppermute | solution.py:271
  4.7 12.3 %all_to_all.5.values_ref = bf16[32,2,640]{2,1,0:T(2,128)(2,1)S(1)} all-to-all(bf16[32,2,640]{2,1,0:T(2,128)(2,1)S(1)} %get-tuple-element.12), channel_id=1, replica_groups=mesh['row'=2,'feat'=16] {'row','feat'}, dimensions={0} | all-to-all | bytes 163840 | tf_op jit(solution)/shard_map/all_to_all | solution.py:268
  17.0 2.7 %sums.1 = (f32[64,136,128]{2,1,0:T(8,128)S(1)}, f32[17,8,128]{2,1,0:T(8,128)S(1)}) custom-call(bf16[32,2,640]{2,1,0:T(2,128)(2,1)S(1)} %all_to_all.5.values_ref, bf16[1040,128]{1,0:T(8,128)(2,1)S(1)} %get-tuple-element.14.bins_ref), custom_call_target="tpu_custom_call" | custom-call | tf_op jit(solution)/shard_map/sums/pallas_call | solution.py:177
  19.7 0.0 collective-permute-done.bins_ref
  19.8 3.1 %gains.1 = (f32[64,8,128]{2,1,0:T(8,128)S(1)}, f32[1,128]{1,0:T(1,128)S(1)}) custom-call(bf16[32,2,640]{2,1,0:T(2,128)(2,1)S(1)} %all_to_all.5.values_ref, s32[1,128]{1,0:T(1,128)S(1)} %get-tuple-element.13.nbins_ref, bf16[1040,128]{1,0:T(8,128)(2,1)S(1)} %collective-permute-done.bins_ref, f32[64,136,128]{2,1,0:T(8,128)S(1)} %get-tuple-element.15.refs_0_, ...), custom_call_target="tpu_custom_call" | custom-call | tf_op jit(solution)/shard_map/gains/pallas_call | solution.py:241
  22.9 0.1 collective-permute-start.1
  23.0 1.0 %collective-permute-done.1 = f32[1,128]{1,0:T(1,128)S(1)} collective-permute-done((f32[1,128]{1,0:T(1,128)S(1)}, f32[1,128]{1,0:T(1,128)S(1)}, u32[]{:S(2)}, u32[]{:S(2)}) %collective-permute-start.1) | collective-permute-done | bytes 544 | tf_op jit(solution)/shard_map/ppermute | solution.py:261
  24.0 0.4 %collective-permute-start.2 = (f32[1,128]{1,0:T(1,128)S(1)}, f32[1,128]{1,0:T(1,128)S(1)}, u32[]{:S(2)}, u32[]{:S(2)}) collective-permute-start(f32[1,128]{1,0:T(1,128)S(1)} %max.12), channel_id=1, source_target_pairs={{0,2},{1,3},{2,0},{3,1},{4,6},{5,7},{6,4},{7,5},{8,10},{9,11},{10,... | collective-permute-start | bytes 1544 | tf_op jit(solution)/shard_map/ppermute | solution.py:261
  24.5 3.1 %collective-permute-done.2 = f32[1,128]{1,0:T(1,128)S(1)} collective-permute-done((f32[1,128]{1,0:T(1,128)S(1)}, f32[1,128]{1,0:T(1,128)S(1)}, u32[]{:S(2)}, u32[]{:S(2)}) %collective-permute-start.2) | collective-permute-done | bytes 544 | tf_op jit(solution)/shard_map/ppermute | solution.py:261
  27.6 0.3 collective-permute-start.3
  27.9 3.3 %collective-permute-done.3 = f32[1,128]{1,0:T(1,128)S(1)} collective-permute-done((f32[1,128]{1,0:T(1,128)S(1)}, f32[1,128]{1,0:T(1,128)S(1)}, u32[]{:S(2)}, u32[]{:S(2)}) %collective-permute-start.3) | collective-permute-done | bytes 544 | tf_op jit(solution)/shard_map/ppermute | solution.py:261
  31.2 0.6 %collective-permute-start.4 = (f32[1,128]{1,0:T(1,128)S(1)}, f32[1,128]{1,0:T(1,128)S(1)}, u32[]{:S(2)}, u32[]{:S(2)}) collective-permute-start(f32[1,128]{1,0:T(1,128)S(1)} %max.14), channel_id=1, source_target_pairs={{0,8},{1,9},{2,10},{3,11},{4,12},{5,13},{6,14},{7,15},{8,0},{9,1},... | collective-permute-start | bytes 1544 | tf_op jit(solution)/shard_map/ppermute | solution.py:261
  31.8 0.2 copy.7
  32.0 0.2 reshape.20
  32.2 3.4 %collective-permute-done.4 = f32[1,128]{1,0:T(1,128)S(1)} collective-permute-done((f32[1,128]{1,0:T(1,128)S(1)}, f32[1,128]{1,0:T(1,128)S(1)}, u32[]{:S(2)}, u32[]{:S(2)}) %collective-permute-start.4) | collective-permute-done | bytes 544 | tf_op jit(solution)/shard_map/ppermute | solution.py:261
  35.7 0.8 %broadcast_divide_fusion = f32[8,8192]{1,0:T(8,128)} fusion(f32[8,8192]{1,0:T(8,128)S(1)} %reshape.20, f32[8]{0:T(128)S(1)} %add_bitcast_fusion), kind=kLoop, calls=%fused_computation | loop fusion | flops 65536 | bytes 524320 | tf_op jit(solution)/shard_map/div | solution.py:279
  (5 shorter events, 0.0 us)
Async XLA Ops:
  1.7 18.0 %collective-permute-start = (bf16[1040,128]{1,0:T(8,128)(2,1)S(1)}, bf16[1040,128]{1,0:T(8,128)(2,1)S(1)}, u32[]{:S(2)}, u32[]{:S(2)}) collective-permute-start(bf16[1040,128]{1,0:T(8,128)(2,1)S(1)} %get-tuple-element.14.bins_ref), channel_id=1, source_target_pairs={{16,0},{0,16},{17,1},{1,17},{18,2},{2,18},{19,3},{3,19},{20,4},{4,... | collective-permute-start | bytes 798728 | tf_op jit(solution)/shard_map/ppermute | solution.py:271
  22.9 1.2 %collective-permute-start.1 = (f32[1,128]{1,0:T(1,128)S(1)}, f32[1,128]{1,0:T(1,128)S(1)}, u32[]{:S(2)}, u32[]{:S(2)}) collective-permute-start(f32[1,128]{1,0:T(1,128)S(1)} %get-tuple-element.18), channel_id=1, source_target_pairs={{0,1},{1,0},{2,3},{3,2},{4,5},{5,4},{6,7},{7,6},{8,9},{9,8},{10,11... | collective-permute-start | bytes 1544 | tf_op jit(solution)/shard_map/ppermute | solution.py:261
  24.0 3.6 %collective-permute-start.2 = (f32[1,128]{1,0:T(1,128)S(1)}, f32[1,128]{1,0:T(1,128)S(1)}, u32[]{:S(2)}, u32[]{:S(2)}) collective-permute-start(f32[1,128]{1,0:T(1,128)S(1)} %max.12), channel_id=1, source_target_pairs={{0,2},{1,3},{2,0},{3,1},{4,6},{5,7},{6,4},{7,5},{8,10},{9,11},{10,... | collective-permute-start | bytes 1544 | tf_op jit(solution)/shard_map/ppermute | solution.py:261
  27.6 3.6 %collective-permute-start.3 = (f32[1,128]{1,0:T(1,128)S(1)}, f32[1,128]{1,0:T(1,128)S(1)}, u32[]{:S(2)}, u32[]{:S(2)}) collective-permute-start(f32[1,128]{1,0:T(1,128)S(1)} %max.13), channel_id=1, source_target_pairs={{0,4},{1,5},{2,6},{3,7},{4,0},{5,1},{6,2},{7,3},{8,12},{9,13},{10,... | collective-permute-start | bytes 1544 | tf_op jit(solution)/shard_map/ppermute | solution.py:261
  31.2 4.5 %collective-permute-start.4 = (f32[1,128]{1,0:T(1,128)S(1)}, f32[1,128]{1,0:T(1,128)S(1)}, u32[]{:S(2)}, u32[]{:S(2)}) collective-permute-start(f32[1,128]{1,0:T(1,128)S(1)} %max.14), channel_id=1, source_target_pairs={{0,8},{1,9},{2,10},{3,11},{4,12},{5,13},{6,14},{7,15},{8,0},{9,1},... | collective-permute-start | bytes 1544 | tf_op jit(solution)/shard_map/ppermute | solution.py:261

commit v4 on v3

--- a/solution.py
+++ b/solution.py
@@ -11,7 +11,8 @@
 BINS = 64
 LEAVES = 16
 LANES = 128
-STEPS = 64
+UNROLLED = 1 << 24
+GRANT = 16 << 20
 ridge = 1.0
 epsilon = 1e-06
 
@@ -149,57 +150,17 @@
     return jnp.dot(weights[...], tables, preferred_element_type=jnp.float32)
 
 
-def sums_kernel(share, features, steps, shift, values_ref, bins_ref, *refs):
+def gain_kernel(share, features, steps, values_ref, nbins_ref, *refs):
     n_row = lax.axis_size("row")
-    earlier, (sums_ref, totals_ref, weights, table) = refs[:-4], refs[-4:]
-    shard = lax.rem(lax.axis_index("row") + shift, n_row)
-    totals = fill_weights(share, shard, values_ref, bins_ref, weights, table)
-    for k in range(17):
-        totals_ref[k] = totals[k] + earlier[1][k] if earlier else totals[k]
-    width = bins_ref.shape[1]
-    copies = width // features
-    bin_of = lax.broadcasted_iota(jnp.int32, (1, width), 1) // features
-
-    def add_group(g, carry):
-        ids = [bin_of + (g * steps + j) * copies for j in range(steps)]
-        sums = left_sums(ids, weights, table)
-        for j in range(steps):
-            part = sums[: 17 * share, j * width : (j + 1) * width]
-            sums_ref[g * steps + j] = part + earlier[0][g * steps + j] if earlier else part
-        return carry
-
-    lax.fori_loop(0, BINS // copies // steps, add_group, 0)
-
-
-def partial_sums(values, bins, share, features, shift, earlier):
-    width = bins.shape[1]
-    rows = values.shape[0] // lax.axis_size("row") * LANES // 2
-    return pl.pallas_call(
-        functools.partial(sums_kernel, share, features, min(STEPS, BINS * features // width), shift),
-        out_shape=(
-            jax.ShapeDtypeStruct((BINS * features // width, 17 * share, width), jnp.float32),
-            jax.ShapeDtypeStruct((17, share, LANES), jnp.float32),
-        ),
-        in_specs=[vmem()] * (2 + len(earlier)),
-        out_specs=(vmem(), vmem()),
-        scratch_shapes=[
-            pltpu.VMEM((padded(share), rows), jnp.bfloat16),
-            pltpu.VMEM((rows, width), jnp.float32),
-        ],
-        compiler_params=pltpu.CompilerParams(vmem_limit_bytes=16 << 20),
-        name="sums",
-    )(values, bins, *earlier)
-
-
-def gain_kernel(share, features, steps, shift, values_ref, nbins_ref, bins_ref, *refs):
-    n_row = lax.axis_size("row")
-    earlier, (gain_ref, best_ref, weights, table) = refs[:-4], refs[-4:]
-    shard = lax.rem(lax.axis_index("row") + shift, n_row)
-    totals = fill_weights(share, shard, values_ref, bins_ref, weights, table)
-    width = bins_ref.shape[1]
+    bins_refs, (gain_ref, best_ref, weights, table) = refs[:-4], refs[-4:]
+    rows, width = table.shape[0] // n_row, table.shape[1]
     full = (share, width)
-    if earlier:
-        totals = [t + earlier[1][k] for k, t in enumerate(totals)]
+    totals = None
+    for s in range(n_row):
+        shard = lax.rem(lax.axis_index("row") + s, n_row)
+        these = pl.ds(s * rows, rows)
+        found = fill_weights(share, shard, values_ref, bins_refs[s], weights.at[:, these], table.at[these, :])
+        totals = found if totals is None else [a + b for a, b in zip(totals, found)]
     totals = [jnp.broadcast_to(jnp.sum(t, axis=1, keepdims=True), full) for t in totals]
 
     def score(sums):
@@ -218,8 +179,6 @@
         sums = left_sums(ids, weights, table)
         for j in range(steps):
             left = [sums[k * share : (k + 1) * share, j * width : (j + 1) * width] for k in range(17)]
-            if earlier:
-                left = [s + earlier[0][g * steps + j, k * share : (k + 1) * share] for k, s in enumerate(left)]
             right = [totals[k] - left[k] for k in range(17)]
             gain = score(left) + score(right) - of_all
             gain = jnp.where(jnp.broadcast_to(ids[j], full) < last, gain, 0.0)
@@ -234,25 +193,29 @@
     best_ref[...] = jnp.max(jnp.where(mine, best, -jnp.inf), axis=0, keepdims=True)
 
 
-def split_gains(values, counts, bins, share, features, shift, earlier):
-    width = bins.shape[1]
+def split_gains(values, counts, bins, share, features):
+    width = bins[0].shape[1]
     copies = width // features
-    rows = values.shape[0] // lax.axis_size("row") * LANES // 2
+    rows = values.shape[0] * LANES // 2
+    steps = BINS // copies
+    while steps % 2 == 0 and rows * width * steps > UNROLLED:
+        steps //= 2
+    held = rows * (4 * width + 2 * padded(share))
     return pl.pallas_call(
-        functools.partial(gain_kernel, share, features, min(STEPS, BINS // copies), shift),
+        functools.partial(gain_kernel, share, features, steps),
         out_shape=(
             jax.ShapeDtypeStruct((BINS // copies, share, width), jnp.float32),
             jax.ShapeDtypeStruct((1, LANES), jnp.float32),
         ),
-        in_specs=[vmem()] * (3 + len(earlier)),
+        in_specs=[vmem()] * (2 + len(bins)),
         out_specs=(vmem(), vmem()),
         scratch_shapes=[
             pltpu.VMEM((padded(share), rows), jnp.bfloat16),
             pltpu.VMEM((rows, width), jnp.float32),
         ],
-        compiler_params=pltpu.CompilerParams(vmem_limit_bytes=16 << 20),
+        compiler_params=pltpu.CompilerParams(vmem_limit_bytes=GRANT + 2 * held),
         name="gains",
-    )(values, counts, bins, *earlier)
+    )(values, counts, *bins)
 
 
 def max_over(x, axis, size):
@@ -270,10 +233,7 @@
     for s in range(1, n_row):
         all_bins.append(lax.ppermute(own, "row", [((i + s) % n_row, i) for i in range(n_row)]))
     share, features = LEAVES // n_row, bins.shape[0]
-    earlier = ()
-    for s in range(n_row - 1):
-        earlier = partial_sums(values, all_bins[s], share, features, s, earlier)
-    gain, best = split_gains(values, counts, all_bins[-1], share, features, n_row - 1, earlier)
+    gain, best = split_gains(values, counts, all_bins, share, features)
     best = max_over(best, "feat", n_feat)
     gain = gain.transpose(1, 0, 2).reshape(share, BINS, features).transpose(0, 2, 1)
     return gain.reshape(share, features * BINS) / (best[0, :share, None] + epsilon)

time: 36.6 us -> 36.3 us (level)
    pallas_call x2 -> x1, Pallas kernels: 5.83 us -> 5.49 us  [split_gains(): pl.pallas_call(functools.partial(gain_kernel, share, features, steps), ou...]
  transfers between devices with their start and end apart: 5 -> 5, of which waited for: 4 -> 4; matrix products, arithmetic and copies ran while one was open for 1% -> 1% of each run, Pallas kernels for 7% -> 0%
where the time goes in v4:
time: 36.3 us; the launch traced here: 36.1 us
  blocking collectives  12.3 us (34%)
  waiting for transfers between devices  10.9 us (30%)
  Pallas kernels  7.18 us (20%)
  starting transfers between devices  4.49 us (12%)
  other arithmetic  0.82 us (2%)
  local copies, waits for them, and re-layouts  0.4 us (1%)
    all_to_all x1, blocking collectives, on_device(): values = lax.all_to_all(copies, ('row', 'feat'), 0, 0)  12.3 us
    ppermute x4, waiting for transfers between devices, max_over(): lax.ppermute(x, axis, [(i, i ^ step) for i in range(size)])  10.9 us
    pallas_call x1, Pallas kernels, split_gains(): pl.pallas_call(functools.partial(gain_kernel, share, features, steps), ou...  5.49 us
    ppermute x1, starting transfers between devices, on_device(): lax.ppermute(own, 'row', [((i + s) % n_row, i) for i in range(n_row)])  3.03 us
    pallas_call x1, Pallas kernels, prepare(): pl.pallas_call(prepare_kernel, out_shape=(jax.ShapeDtypeStruct((lines + t...  1.69 us
    ppermute x4, starting transfers between devices, max_over(): lax.ppermute(x, axis, [(i, i ^ step) for i in range(size)])  1.46 us
    div x1, other arithmetic, on_device(): gain.reshape(share, features * BINS) / (best[0, :share, None] + epsilon)  0.8 us
  transfers between devices with their start and end apart: 5, of which 4 were waited for; matrix products, arithmetic and copies ran while one was open for 1% of the time, Pallas kernels for 0%

profile of v4, /device:TPU:0, one launch (start us, length us, event | category | flops | bytes accessed | tf_op | source)
XLA Modules:
  0.0 36.1 jit_solution(11136034543516943473)
XLA Ops:
  0.0 1.7 %prepare.1 = (bf16[1040,128]{1,0:T(8,128)(2,1)S(1)}, bf16[32,2,640]{2,1,0:T(2,128)(2,1)S(1)}, s32[1,128]{1,0:T(1,128)S(1)}) custom-call(s32[128,1024]{1,0:T(8,128)} %refs_0_.1, s32[8,128]{1,0:T(8,128)} %bitcast.9, bf16[64,1000]{1,0:T(8,128)(2,1)} %refs_2_.1, s32[1,64]{1,0:T(1,128)} %bitcast.10, bf16[16,1000]{1,0:T(8,128)(2,1)} %bitcast.8, s32[1,128]{1,0:T(1,128)} %bitcast.11), custom_call_target="tpu_custom_call" | custom-call | tf_op jit(solution)/shard_map/prepare/pallas_call | solution.py:91
  1.7 3.0 %collective-permute-start = (bf16[1040,128]{1,0:T(8,128)(2,1)S(1)}, bf16[1040,128]{1,0:T(8,128)(2,1)S(1)}, u32[]{:S(2)}, u32[]{:S(2)}) collective-permute-start(bf16[1040,128]{1,0:T(8,128)(2,1)S(1)} %get-tuple-element.12.refs_0_), channel_id=1, source_target_pairs={{16,0},{0,16},{17,1},{1,17},{18,2},{2,18},{19,3},{3,19},{20,4},{4,... | collective-permute-start | bytes 798728 | tf_op jit(solution)/shard_map/ppermute | solution.py:234
  4.7 12.3 %all_to_all.5.values_ref = bf16[32,2,640]{2,1,0:T(2,128)(2,1)S(1)} all-to-all(bf16[32,2,640]{2,1,0:T(2,128)(2,1)S(1)} %get-tuple-element.10), channel_id=1, replica_groups=mesh['row'=2,'feat'=16] {'row','feat'}, dimensions={0} | all-to-all | bytes 163840 | tf_op jit(solution)/shard_map/all_to_all | solution.py:231
  17.0 0.0 collective-permute-done.refs_1_
  17.0 5.5 %gains.1 = (f32[64,8,128]{2,1,0:T(8,128)S(1)}, f32[1,128]{1,0:T(1,128)S(1)}) custom-call(bf16[32,2,640]{2,1,0:T(2,128)(2,1)S(1)} %all_to_all.5.values_ref, s32[1,128]{1,0:T(1,128)S(1)} %get-tuple-element.11.nbins_ref, bf16[1040,128]{1,0:T(8,128)(2,1)S(1)} %get-tuple-element.12.refs_0_, bf16[1040,128]{1,0:T(8,128)(2,1)S(1)} %collective-permute-done.refs_1_), custom_call_target="tpu_custom_call" | custom-call | tf_op jit(solution)/shard_map/gains/pallas_call | solution.py:204
  22.5 0.1 collective-permute-start.1
  22.6 1.0 %collective-permute-done.1 = f32[1,128]{1,0:T(1,128)S(1)} collective-permute-done((f32[1,128]{1,0:T(1,128)S(1)}, f32[1,128]{1,0:T(1,128)S(1)}, u32[]{:S(2)}, u32[]{:S(2)}) %collective-permute-start.1) | collective-permute-done | bytes 544 | tf_op jit(solution)/shard_map/ppermute | solution.py:224
  23.7 0.4 %collective-permute-start.2 = (f32[1,128]{1,0:T(1,128)S(1)}, f32[1,128]{1,0:T(1,128)S(1)}, u32[]{:S(2)}, u32[]{:S(2)}) collective-permute-start(f32[1,128]{1,0:T(1,128)S(1)} %max.12), channel_id=1, source_target_pairs={{0,2},{1,3},{2,0},{3,1},{4,6},{5,7},{6,4},{7,5},{8,10},{9,11},{10,... | collective-permute-start | bytes 1544 | tf_op jit(solution)/shard_map/ppermute | solution.py:224
  24.1 3.1 %collective-permute-done.2 = f32[1,128]{1,0:T(1,128)S(1)} collective-permute-done((f32[1,128]{1,0:T(1,128)S(1)}, f32[1,128]{1,0:T(1,128)S(1)}, u32[]{:S(2)}, u32[]{:S(2)}) %collective-permute-start.2) | collective-permute-done | bytes 544 | tf_op jit(solution)/shard_map/ppermute | solution.py:224
  27.3 0.3 collective-permute-start.3
  27.6 3.3 %collective-permute-done.3 = f32[1,128]{1,0:T(1,128)S(1)} collective-permute-done((f32[1,128]{1,0:T(1,128)S(1)}, f32[1,128]{1,0:T(1,128)S(1)}, u32[]{:S(2)}, u32[]{:S(2)}) %collective-permute-start.3) | collective-permute-done | bytes 544 | tf_op jit(solution)/shard_map/ppermute | solution.py:224
  30.8 0.6 %collective-permute-start.4 = (f32[1,128]{1,0:T(1,128)S(1)}, f32[1,128]{1,0:T(1,128)S(1)}, u32[]{:S(2)}, u32[]{:S(2)}) collective-permute-start(f32[1,128]{1,0:T(1,128)S(1)} %max.14), channel_id=1, source_target_pairs={{0,8},{1,9},{2,10},{3,11},{4,12},{5,13},{6,14},{7,15},{8,0},{9,1},... | collective-permute-start | bytes 1544 | tf_op jit(solution)/shard_map/ppermute | solution.py:224
  31.5 0.2 copy.7
  31.7 0.2 reshape.20
  31.9 3.4 %collective-permute-done.4 = f32[1,128]{1,0:T(1,128)S(1)} collective-permute-done((f32[1,128]{1,0:T(1,128)S(1)}, f32[1,128]{1,0:T(1,128)S(1)}, u32[]{:S(2)}, u32[]{:S(2)}) %collective-permute-start.4) | collective-permute-done | bytes 544 | tf_op jit(solution)/shard_map/ppermute | solution.py:224
  35.3 0.8 %broadcast_divide_fusion = f32[8,8192]{1,0:T(8,128)} fusion(f32[8,8192]{1,0:T(8,128)S(1)} %reshape.20, f32[8]{0:T(128)S(1)} %add_bitcast_fusion), kind=kLoop, calls=%fused_computation | loop fusion | flops 65536 | bytes 524320 | tf_op jit(solution)/shard_map/div | solution.py:239
  (5 shorter events, 0.0 us)
Async XLA Ops:
  1.7 15.3 %collective-permute-start = (bf16[1040,128]{1,0:T(8,128)(2,1)S(1)}, bf16[1040,128]{1,0:T(8,128)(2,1)S(1)}, u32[]{:S(2)}, u32[]{:S(2)}) collective-permute-start(bf16[1040,128]{1,0:T(8,128)(2,1)S(1)} %get-tuple-element.12.refs_0_), channel_id=1, source_target_pairs={{16,0},{0,16},{17,1},{1,17},{18,2},{2,18},{19,3},{3,19},{20,4},{4,... | collective-permute-start | bytes 798728 | tf_op jit(solution)/shard_map/ppermute | solution.py:234
  22.5 1.2 %collective-permute-start.1 = (f32[1,128]{1,0:T(1,128)S(1)}, f32[1,128]{1,0:T(1,128)S(1)}, u32[]{:S(2)}, u32[]{:S(2)}) collective-permute-start(f32[1,128]{1,0:T(1,128)S(1)} %get-tuple-element.14), channel_id=1, source_target_pairs={{0,1},{1,0},{2,3},{3,2},{4,5},{5,4},{6,7},{7,6},{8,9},{9,8},{10,11... | collective-permute-start | bytes 1544 | tf_op jit(solution)/shard_map/ppermute | solution.py:224
  23.7 3.6 %collective-permute-start.2 = (f32[1,128]{1,0:T(1,128)S(1)}, f32[1,128]{1,0:T(1,128)S(1)}, u32[]{:S(2)}, u32[]{:S(2)}) collective-permute-start(f32[1,128]{1,0:T(1,128)S(1)} %max.12), channel_id=1, source_target_pairs={{0,2},{1,3},{2,0},{3,1},{4,6},{5,7},{6,4},{7,5},{8,10},{9,11},{10,... | collective-permute-start | bytes 1544 | tf_op jit(solution)/shard_map/ppermute | solution.py:224
  27.3 3.6 %collective-permute-start.3 = (f32[1,128]{1,0:T(1,128)S(1)}, f32[1,128]{1,0:T(1,128)S(1)}, u32[]{:S(2)}, u32[]{:S(2)}) collective-permute-start(f32[1,128]{1,0:T(1,128)S(1)} %max.13), channel_id=1, source_target_pairs={{0,4},{1,5},{2,6},{3,7},{4,0},{5,1},{6,2},{7,3},{8,12},{9,13},{10,... | collective-permute-start | bytes 1544 | tf_op jit(solution)/shard_map/ppermute | solution.py:224
  30.8 4.5 %collective-permute-start.4 = (f32[1,128]{1,0:T(1,128)S(1)}, f32[1,128]{1,0:T(1,128)S(1)}, u32[]{:S(2)}, u32[]{:S(2)}) collective-permute-start(f32[1,128]{1,0:T(1,128)S(1)} %max.14), channel_id=1, source_target_pairs={{0,8},{1,9},{2,10},{3,11},{4,12},{5,13},{6,14},{7,15},{8,0},{9,1},... | collective-permute-start | bytes 1544 | tf_op jit(solution)/shard_map/ppermute | solution.py:224

commit v5 on v4

--- a/solution.py
+++ b/solution.py
@@ -190,10 +190,11 @@
     best = lax.fori_loop(0, count, add_group, jnp.full(full, -jnp.inf, jnp.float32))
     best = jnp.broadcast_to(jnp.max(best, axis=1, keepdims=True), (share, LANES))
     mine = lax.broadcasted_iota(jnp.int32, (share, LANES), 0) == lax.broadcasted_iota(jnp.int32, (share, LANES), 1)
-    best_ref[...] = jnp.max(jnp.where(mine, best, -jnp.inf), axis=0, keepdims=True)
-
-
-def split_gains(values, counts, bins, share, features):
+    best = jnp.max(jnp.where(mine, best, -jnp.inf), axis=0, keepdims=True)
+    best_ref[...] = jnp.broadcast_to(best[None], best_ref.shape)
+
+
+def split_gains(values, counts, bins, share, features, destinations):
     width = bins[0].shape[1]
     copies = width // features
     rows = values.shape[0] * LANES // 2
@@ -205,7 +206,7 @@
         functools.partial(gain_kernel, share, features, steps),
         out_shape=(
             jax.ShapeDtypeStruct((BINS // copies, share, width), jnp.float32),
-            jax.ShapeDtypeStruct((1, LANES), jnp.float32),
+            jax.ShapeDtypeStruct((destinations, 1, LANES), jnp.float32),
         ),
         in_specs=[vmem()] * (2 + len(bins)),
         out_specs=(vmem(), vmem()),
@@ -218,14 +219,6 @@
     )(values, counts, *bins)
 
 
-def max_over(x, axis, size):
-    step = 1
-    while step < size:
-        x = jnp.maximum(x, lax.ppermute(x, axis, [(i, i ^ step) for i in range(size)]))
-        step *= 2
-    return x
-
-
 def on_device(n_row, n_feat, logits, labels, projection, bins, nbins, leaf):
     own, copies, counts = prepare(bins, leaf, logits, labels, projection, nbins, n_row * n_feat)
     values = lax.all_to_all(copies, ("row", "feat"), 0, 0)
@@ -233,10 +226,11 @@
     for s in range(1, n_row):
         all_bins.append(lax.ppermute(own, "row", [((i + s) % n_row, i) for i in range(n_row)]))
     share, features = LEAVES // n_row, bins.shape[0]
-    gain, best = split_gains(values, counts, all_bins, share, features)
-    best = max_over(best, "feat", n_feat)
+    gain, best = split_gains(values, counts, all_bins, share, features, n_feat)
     gain = gain.transpose(1, 0, 2).reshape(share, BINS, features).transpose(0, 2, 1)
-    return gain.reshape(share, features * BINS) / (best[0, :share, None] + epsilon)
+    gain, best = lax.optimization_barrier((gain.reshape(share, features * BINS), best))
+    best = lax.all_to_all(best, "feat", 0, 0)
+    return gain / (jnp.max(best, axis=(0, 1))[:share, None] + epsilon)
 
 
 def solution(mesh):

time: 36.3 us -> 33 us (0.909)
  waiting for transfers between devices: 10.9 us -> 0.01 us
  blocking collectives: 12.3 us -> 21.3 us
  starting transfers between devices: 4.49 us -> 3.03 us
    ppermute x4 -> x0, waiting for transfers between devices: 10.9 us -> none  [max_over(): lax.ppermute(x, axis, [(i, i ^ step) for i in range(size)])]
    all_to_all x0 -> x1, blocking collectives: none -> 9 us  [on_device(): best = lax.all_to_all(best, 'feat', 0, 0)]
    ppermute x4 -> x0, starting transfers between devices: 1.46 us -> none  [max_over(): lax.ppermute(x, axis, [(i, i ^ step) for i in range(size)])]
  transfers between devices with their start and end apart: 5 -> 1, of which waited for: 4 -> 0; matrix products, arithmetic and copies ran while one was open for 1% -> 0% of each run, Pallas kernels for 0% -> 0%
where the time goes in v5:
time: 33 us; the launch traced here: 32.8 us
  blocking collectives  21.3 us (65%)
  Pallas kernels  7.19 us (22%)
  starting transfers between devices  3.03 us (9%)
  other arithmetic  0.84 us (3%)
  local copies, waits for them, and re-layouts  0.4 us (1%)
    all_to_all x1, blocking collectives, on_device(): values = lax.all_to_all(copies, ('row', 'feat'), 0, 0)  12.3 us
    all_to_all x1, blocking collectives, on_device(): best = lax.all_to_all(best, 'feat', 0, 0)  9 us
    pallas_call x1, Pallas kernels, split_gains(): pl.pallas_call(functools.partial(gain_kernel, share, features, steps), ou...  5.5 us
    ppermute x1, starting transfers between devices, on_device(): lax.ppermute(own, 'row', [((i + s) % n_row, i) for i in range(n_row)])  3.03 us
    pallas_call x1, Pallas kernels, prepare(): pl.pallas_call(prepare_kernel, out_shape=(jax.ShapeDtypeStruct((lines + t...  1.69 us
    div x1, other arithmetic, on_device(): return gain / (jnp.max(best, axis=(0, 1))[:share, None] + epsilon)  0.8 us
  transfers between devices with their start and end apart: 1, of which 0 were waited for; matrix products, arithmetic and copies ran while one was open for 0% of the time, Pallas kernels for 0%

profile of v5, /device:TPU:0, one launch (start us, length us, event | category | flops | bytes accessed | tf_op | source)
XLA Modules:
  0.0 32.8 jit_solution(3784789836028783719)
XLA Ops:
  0.0 1.7 %prepare.1 = (bf16[1040,128]{1,0:T(8,128)(2,1)S(1)}, bf16[32,2,640]{2,1,0:T(2,128)(2,1)S(1)}, s32[1,128]{1,0:T(1,128)S(1)}) custom-call(s32[128,1024]{1,0:T(8,128)} %refs_0_.1, s32[8,128]{1,0:T(8,128)} %bitcast.7, bf16[64,1000]{1,0:T(8,128)(2,1)} %refs_2_.1, s32[1,64]{1,0:T(1,128)} %bitcast.8, bf16[16,1000]{1,0:T(8,128)(2,1)} %bitcast.6, s32[1,128]{1,0:T(1,128)} %bitcast.9), custom_call_target="tpu_custom_call" | custom-call | tf_op jit(solution)/shard_map/prepare/pallas_call | solution.py:91
  1.7 3.0 %collective-permute-start = (bf16[1040,128]{1,0:T(8,128)(2,1)S(1)}, bf16[1040,128]{1,0:T(8,128)(2,1)S(1)}, u32[]{:S(2)}, u32[]{:S(2)}) collective-permute-start(bf16[1040,128]{1,0:T(8,128)(2,1)S(1)} %get-tuple-element.14.refs_0_), channel_id=1, source_target_pairs={{16,0},{0,16},{17,1},{1,17},{18,2},{2,18},{19,3},{3,19},{20,4},{4,... | collective-permute-start | bytes 798728 | tf_op jit(solution)/shard_map/ppermute | solution.py:227
  4.7 12.3 %all_to_all.10.values_ref = bf16[32,2,640]{2,1,0:T(2,128)(2,1)S(1)} all-to-all(bf16[32,2,640]{2,1,0:T(2,128)(2,1)S(1)} %get-tuple-element.12), channel_id=1, replica_groups=mesh['row'=2,'feat'=16] {'row','feat'}, dimensions={0} | all-to-all | bytes 163840 | tf_op jit(solution)/shard_map/all_to_all | solution.py:224
  17.0 0.0 collective-permute-done.refs_1_
  17.0 5.5 %gains.1 = (f32[64,8,128]{2,1,0:T(8,128)S(1)}, f32[16,1,128]{2,1,0:T(1,128)S(1)}) custom-call(bf16[32,2,640]{2,1,0:T(2,128)(2,1)S(1)} %all_to_all.10.values_ref, s32[1,128]{1,0:T(1,128)S(1)} %get-tuple-element.13.nbins_ref, bf16[1040,128]{1,0:T(8,128)(2,1)S(1)} %get-tuple-element.14.refs_0_, bf16[1040,128]{1,0:T(8,128)(2,1)S(1)} %collective-permute-done.refs_1_), custom_call_target="tpu_custom_call" | custom-call | tf_op jit(solution)/shard_map/gains/pallas_call | solution.py:205
  22.5 0.2 copy.7
  22.8 0.2 reshape.13
  22.9 9.0 %all_to_all.11 = f32[16,1,128]{2,1,0:T(1,128)S(1)} all-to-all(f32[16,1,128]{2,1,0:T(1,128)S(1)} %get-tuple-element.18), channel_id=1, replica_groups=mesh['row'=2,'feat'=16] {'feat'}, dimensions={0} | all-to-all | bytes 16384 | tf_op jit(solution)/shard_map/all_to_all | solution.py:232
  32.0 0.8 %broadcast_divide_fusion = f32[8,8192]{1,0:T(8,128)} fusion(f32[8,8192]{1,0:T(8,128)S(1)} %reshape.13, f32[8]{0:T(128)S(1)} %slice_add_fusion), kind=kLoop, calls=%fused_computation | loop fusion | flops 65536 | bytes 524320 | tf_op jit(solution)/shard_map/div | solution.py:233
  (2 shorter events, 0.0 us)
Async XLA Ops:
  1.7 15.3 %collective-permute-start = (bf16[1040,128]{1,0:T(8,128)(2,1)S(1)}, bf16[1040,128]{1,0:T(8,128)(2,1)S(1)}, u32[]{:S(2)}, u32[]{:S(2)}) collective-permute-start(bf16[1040,128]{1,0:T(8,128)(2,1)S(1)} %get-tuple-element.14.refs_0_), channel_id=1, source_target_pairs={{16,0},{0,16},{17,1},{1,17},{18,2},{2,18},{19,3},{3,19},{20,4},{4,... | collective-permute-start | bytes 798728 | tf_op jit(solution)/shard_map/ppermute | solution.py:227

commit v6 on v5

--- a/solution.py
+++ b/solution.py
@@ -12,6 +12,8 @@
 LEAVES = 16
 LANES = 128
 UNROLLED = 1 << 24
+HALF = 38
+QUARTER = 52
 GRANT = 16 << 20
 ridge = 1.0
 epsilon = 1e-06
@@ -142,17 +144,18 @@
     return totals
 
 
-def left_sums(ids, weights, table):
+def left_sums(ids, weights, tables):
     one, zero = jnp.bfloat16(1.0), jnp.bfloat16(0.0)
-    bins = table[...].astype(jnp.bfloat16)
+    bins = {id(ref): ref[...].astype(jnp.bfloat16) for ref in tables}
     ids = [i.astype(jnp.float32).astype(jnp.bfloat16) for i in ids]
-    tables = jnp.concatenate([jnp.where(bins <= i, one, zero) for i in ids], axis=1)
-    return jnp.dot(weights[...], tables, preferred_element_type=jnp.float32)
+    hot = [jnp.where(bins[id(ref)] <= i, one, zero) for i, ref in zip(ids, tables)]
+    return jnp.dot(weights[...], jnp.concatenate(hot, axis=1), preferred_element_type=jnp.float32)
 
 
 def gain_kernel(share, features, steps, values_ref, nbins_ref, *refs):
     n_row = lax.axis_size("row")
-    bins_refs, (gain_ref, best_ref, weights, table) = refs[:-4], refs[-4:]
+    bins_refs, (gain_ref, best_ref, weights, table, most_ref) = refs[:n_row], refs[n_row : n_row + 5]
+    sorted_refs = refs[n_row + 5 :]
     rows, width = table.shape[0] // n_row, table.shape[1]
     full = (share, width)
     totals = None
@@ -174,20 +177,70 @@
     bin_of = lax.broadcasted_iota(jnp.int32, (1, width), 1) // features
     last = jnp.broadcast_to(nbins_ref[...] - 1, full)
 
+    def gain_of(sums, j):
+        left = [sums[k * share : (k + 1) * share, j * width : (j + 1) * width] for k in range(17)]
+        right = [totals[k] - left[k] for k in range(17)]
+        return score(left) + score(right) - of_all
+
+    def keep(at, ids, gain, best):
+        gain = jnp.where(jnp.broadcast_to(ids, full) < last, gain, 0.0)
+        gain_ref[at] = gain
+        return jnp.maximum(best, gain)
+
     def add_group(g, best):
         ids = [bin_of + (g * steps + j) * copies for j in range(steps)]
-        sums = left_sums(ids, weights, table)
+        sums = left_sums(ids, weights, [table] * steps)
         for j in range(steps):
-            left = [sums[k * share : (k + 1) * share, j * width : (j + 1) * width] for k in range(17)]
-            right = [totals[k] - left[k] for k in range(17)]
-            gain = score(left) + score(right) - of_all
-            gain = jnp.where(jnp.broadcast_to(ids[j], full) < last, gain, 0.0)
-            gain_ref[g * steps + j] = gain
-            best = jnp.maximum(best, gain)
+            best = keep(g * steps + j, ids[j], gain_of(sums, j), best)
         return best
 
-    count = BINS // copies // steps
-    best = lax.fori_loop(0, count, add_group, jnp.full(full, -jnp.inf, jnp.float32))
+    lowest = jnp.full(full, -jnp.inf, jnp.float32)
+
+    def every_feature():
+        most_ref[...] = lax.fori_loop(0, BINS // copies // steps, add_group, lowest)
+
+    if not sorted_refs:
+        every_feature()
+    else:
+        halves, quarters = sorted_refs
+        square = (LANES, LANES)
+        counts = jnp.broadcast_to(nbins_ref[...].astype(jnp.float32), square)
+        other = jnp.transpose(counts)
+        index = lax.broadcasted_iota(jnp.int32, square, 0)
+        lane = lax.broadcasted_iota(jnp.int32, square, 1)
+        ahead = jnp.where(other > counts, 1.0, jnp.where((other == counts) & (index < lane), 1.0, 0.0))
+        rank = jnp.sum(ahead, axis=0, keepdims=True)
+        turned = jnp.transpose(jnp.broadcast_to(rank, square)).astype(jnp.int32)
+        rank = jnp.broadcast_to(rank.astype(jnp.int32), full)
+        few = (last[:1] > HALF) & (rank[:1] >= LANES // 2) | (last[:1] > QUARTER) & (rank[:1] >= LANES // 4)
+        fits = jnp.sum(jnp.where(few, 1, 0)) == 0
+
+        @pl.when(fits)
+        def _():
+            bins = table[...].astype(jnp.bfloat16)
+            for part, ref in ((2, halves), (4, quarters)):
+                pick = jnp.where(turned == lax.rem(lane, LANES // part), 1.0, 0.0).astype(jnp.bfloat16)
+                ref[...] = jnp.dot(bins, pick, preferred_element_type=jnp.float32)
+            tiles = [(b, 1, table) for b in range(HALF)]
+            tiles += [(b, 2, halves) for b in range(HALF, QUARTER, 2)]
+            tiles += [(b, 4, quarters) for b in range(QUARTER, BINS, 4)]
+            lanes = lax.broadcasted_iota(jnp.int32, (1, LANES), 1)
+            ids = [b + lanes // (LANES // part) for b, part, _ in tiles]
+            sums = left_sums(ids, weights, [ref for _, _, ref in tiles])
+            best = lowest
+            for j, (b, part, _) in enumerate(tiles):
+                gain = gain_of(sums, j)
+                for sub in range(part):
+                    own = gain
+                    if part > 1:
+                        at = jnp.minimum(rank + sub * (LANES // part), LANES - 1)
+                        own = jnp.take_along_axis(gain, at, axis=1, mode="promise_in_bounds")
+                    best = keep(b + sub, jnp.full((1, LANES), b + sub, jnp.int32), own, best)
+            most_ref[...] = best
+
+        pl.when(jnp.logical_not(fits))(every_feature)
+
+    best = most_ref[...]
     best = jnp.broadcast_to(jnp.max(best, axis=1, keepdims=True), (share, LANES))
     mine = lax.broadcasted_iota(jnp.int32, (share, LANES), 0) == lax.broadcasted_iota(jnp.int32, (share, LANES), 1)
     best = jnp.max(jnp.where(mine, best, -jnp.inf), axis=0, keepdims=True)
@@ -202,6 +255,7 @@
     while steps % 2 == 0 and rows * width * steps > UNROLLED:
         steps //= 2
     held = rows * (4 * width + 2 * padded(share))
+    sort = features == LANES and steps == BINS
     return pl.pallas_call(
         functools.partial(gain_kernel, share, features, steps),
         out_shape=(
@@ -213,7 +267,9 @@
         scratch_shapes=[
             pltpu.VMEM((padded(share), rows), jnp.bfloat16),
             pltpu.VMEM((rows, width), jnp.float32),
-        ],
+            pltpu.VMEM((share, width), jnp.float32),
+        ]
+        + [pltpu.VMEM((rows, width), jnp.float32)] * (2 if sort else 0),
         compiler_params=pltpu.CompilerParams(vmem_limit_bytes=GRANT + 2 * held),
         name="gains",
     )(values, counts, *bins)

time: 33 us -> 32.3 us (0.979)
  Pallas kernels: 7.19 us -> 6.51 us
    pallas_call x1, Pallas kernels: 5.5 us -> 4.82 us  [split_gains(): pl.pallas_call(functools.partial(gain_kernel, share, features, steps), ou...]
where the time goes in v6:
time: 32.3 us; the launch traced here: 32.1 us
  blocking collectives  21.3 us (66%)
  Pallas kernels  6.51 us (20%)
  starting transfers between devices  3.03 us (9%)
  other arithmetic  0.84 us (3%)
  local copies, waits for them, and re-layouts  0.41 us (1%)
    all_to_all x1, blocking collectives, on_device(): values = lax.all_to_all(copies, ('row', 'feat'), 0, 0)  12.3 us
    all_to_all x1, blocking collectives, on_device(): best = lax.all_to_all(best, 'feat', 0, 0)  9 us
    pallas_call x1, Pallas kernels, split_gains(): pl.pallas_call(functools.partial(gain_kernel, share, features, steps), ou...  4.82 us
    ppermute x1, starting transfers between devices, on_device(): lax.ppermute(own, 'row', [((i + s) % n_row, i) for i in range(n_row)])  3.03 us
    pallas_call x1, Pallas kernels, prepare(): pl.pallas_call(prepare_kernel, out_shape=(jax.ShapeDtypeStruct((lines + t...  1.69 us
    div x1, other arithmetic, on_device(): return gain / (jnp.max(best, axis=(0, 1))[:share, None] + epsilon)  0.8 us
  transfers between devices with their start and end apart: 1, of which 0 were waited for; matrix products, arithmetic and copies ran while one was open for 0% of the time, Pallas kernels for 0%

profile of v6, /device:TPU:0, one launch (start us, length us, event | category | flops | bytes accessed | tf_op | source)
XLA Modules:
  0.0 32.1 jit_solution(2238022874616953330)
XLA Ops:
  0.0 1.7 %prepare.1 = (bf16[1040,128]{1,0:T(8,128)(2,1)S(1)}, bf16[32,2,640]{2,1,0:T(2,128)(2,1)S(1)}, s32[1,128]{1,0:T(1,128)S(1)}) custom-call(s32[128,1024]{1,0:T(8,128)} %refs_0_.1, s32[8,128]{1,0:T(8,128)} %bitcast.7, bf16[64,1000]{1,0:T(8,128)(2,1)} %refs_2_.1, s32[1,64]{1,0:T(1,128)} %bitcast.8, bf16[16,1000]{1,0:T(8,128)(2,1)} %bitcast.6, s32[1,128]{1,0:T(1,128)} %bitcast.9), custom_call_target="tpu_custom_call" | custom-call | tf_op jit(solution)/shard_map/prepare/pallas_call | solution.py:93
  1.7 3.0 %collective-permute-start = (bf16[1040,128]{1,0:T(8,128)(2,1)S(1)}, bf16[1040,128]{1,0:T(8,128)(2,1)S(1)}, u32[]{:S(2)}, u32[]{:S(2)}) collective-permute-start(bf16[1040,128]{1,0:T(8,128)(2,1)S(1)} %get-tuple-element.14.refs_0_), channel_id=1, source_target_pairs={{16,0},{0,16},{17,1},{1,17},{18,2},{2,18},{19,3},{3,19},{20,4},{4,... | collective-permute-start | bytes 798728 | tf_op jit(solution)/shard_map/ppermute | solution.py:283
  4.7 12.3 %all_to_all.10.values_ref = bf16[32,2,640]{2,1,0:T(2,128)(2,1)S(1)} all-to-all(bf16[32,2,640]{2,1,0:T(2,128)(2,1)S(1)} %get-tuple-element.12), channel_id=1, replica_groups=mesh['row'=2,'feat'=16] {'row','feat'}, dimensions={0} | all-to-all | bytes 163840 | tf_op jit(solution)/shard_map/all_to_all | solution.py:280
  17.0 0.0 collective-permute-done.refs_1_
  17.0 4.8 %gains.1 = (f32[64,8,128]{2,1,0:T(8,128)S(1)}, f32[16,1,128]{2,1,0:T(1,128)S(1)}) custom-call(bf16[32,2,640]{2,1,0:T(2,128)(2,1)S(1)} %all_to_all.10.values_ref, s32[1,128]{1,0:T(1,128)S(1)} %get-tuple-element.13.nbins_ref, bf16[1040,128]{1,0:T(8,128)(2,1)S(1)} %get-tuple-element.14.refs_0_, bf16[1040,128]{1,0:T(8,128)(2,1)S(1)} %collective-permute-done.refs_1_), custom_call_target="tpu_custom_call" | custom-call | tf_op jit(solution)/shard_map/gains/pallas_call | solution.py:259
  21.9 0.2 copy.7
  22.1 0.2 reshape.13
  22.3 9.0 %all_to_all.11 = f32[16,1,128]{2,1,0:T(1,128)S(1)} all-to-all(f32[16,1,128]{2,1,0:T(1,128)S(1)} %get-tuple-element.18), channel_id=1, replica_groups=mesh['row'=2,'feat'=16] {'feat'}, dimensions={0} | all-to-all | bytes 16384 | tf_op jit(solution)/shard_map/all_to_all | solution.py:288
  31.3 0.8 %broadcast_divide_fusion = f32[8,8192]{1,0:T(8,128)} fusion(f32[8,8192]{1,0:T(8,128)S(1)} %reshape.13, f32[8]{0:T(128)S(1)} %slice_add_fusion), kind=kLoop, calls=%fused_computation | loop fusion | flops 65536 | bytes 524320 | tf_op jit(solution)/shard_map/div | solution.py:289
  (2 shorter events, 0.0 us)
Async XLA Ops:
  1.7 15.3 %collective-permute-start = (bf16[1040,128]{1,0:T(8,128)(2,1)S(1)}, bf16[1040,128]{1,0:T(8,128)(2,1)S(1)}, u32[]{:S(2)}, u32[]{:S(2)}) collective-permute-start(bf16[1040,128]{1,0:T(8,128)(2,1)S(1)} %get-tuple-element.14.refs_0_), channel_id=1, source_target_pairs={{16,0},{0,16},{17,1},{1,17},{18,2},{2,18},{19,3},{3,19},{20,4},{4,... | collective-permute-start | bytes 798728 | tf_op jit(solution)/shard_map/ppermute | solution.py:283
